TPU v7x, 128 devices: a whole 4x4x4 slice. The times are simulated.
128 devices in a mesh: det: 4 (over x), tm: 32 (over y, z, core).
Axes of the slice: x: 4, y: 4, z: 4, core: 2. Of those that a mesh axis runs over, the one named last changes fastest.
Arguments:
- tod: bfloat16 [8, 2048, 256], P('det', 'tm'), may hold values from -6 to 6
- pointing: bfloat16 [8, 2048, 256, 128], P('det', 'tm'), may hold values from -0.5 to 0.5
- weights: float32 [8, 2048, 256], P('det', 'tm'), may hold values from 0.2 to 2
- tile_ids: int32 [8, 2048], P('det', 'tm'), may hold values from 0 to 2047, as said below
- offsets: int32 [8, 2048], P('det', 'tm'), may hold values from 0 to 896
- neighbours: int32 [2048, 2], P(('det', 'tm')), may hold values from 0 to 2047, as said below
Outputs:
- solution: float32 [2048, 1024], P(('det', 'tm'))
- residual: float32 [2048, 1024], P(('det', 'tm'))
Inputs may be any that keep to these rules, and one draw needn't show every extreme that they name: `tile_ids`: take the blocks of one device (detectors of one index of det, time blocks of one index of tm) in detector-major order: each consecutive run of 2 of them names tiles of one owner device (tile // 16), different runs name different owners, so at most 2 blocks of one device name one owner, and this is reached; some owner is named by 2 blocks of every device. The tiles form one cycle: neighbours[neighbours[t,1],0] == t for every tile t.
All inputs are finite; a program needn't handle non-finite values.
Results may differ from a plain program's by a relative error of at most 0.017.
Values may be sent and summed in bfloat16 or wider, within the bound.
No kernel may reach another device: no remote copies, remote signals or barrier semaphores. Data moves between devices by JAX's collectives and lax.ppermute only.
A program may use at most 64 MiB of HBM per device.

v0:
```python
import jax
import jax.numpy as jnp
from jax import lax
from jax.sharding import Mesh
from jax.sharding import PartitionSpec as P

SAMP = 256
FOOT = 128
TILE_PIX = 1024
ITERS = 2
DET_TM = ("det", "tm_0", "tm_1", "tm_2")
TM = ("tm_0", "tm_1", "tm_2")


smooth_weight = 2.0
ridge_weight = 0.5


def split_up(x, dim, length):
    lengths = x.shape
    pieces = x.reshape(*lengths[:dim], length, lengths[dim] // length, *lengths[dim + 1 :])
    return jnp.moveaxis(pieces, dim, 0)


def laid_out(pieces, dim):
    lengths = list(pieces.shape[1:])
    lengths[dim] *= pieces.shape[0]
    return jnp.moveaxis(pieces, 0, dim).reshape(lengths)


def exchange_in_order(pieces, axes, sequence):
    inside = pieces.shape[1:]
    result = pieces.reshape(*(lax.axis_size(a) for a in axes), *inside)
    for k in sequence:
        result = lax.all_to_all(result, axes[k], k, k, tiled=True)
    return result.reshape(-1, *inside)


def exchange_by_chip(x, groups, sequence, split_dim, concat_dim):
    length = lax.axis_size(groups[0]) * lax.axis_size(groups[1])
    pieces = split_up(x, split_dim, length)
    return laid_out(exchange_in_order(pieces, groups, sequence), concat_dim)


def by_axis(x, axes):
    for axis in axes:
        x = lax.psum(x, axis)
    return x


def per_device(tod, pointing, weights, tile_ids, offsets, neighbours):
    device_total_count = lax.axis_size(DET_TM)
    tile_count = neighbours.shape[0]
    beam_blocks = pointing.reshape(-1, SAMP, FOOT)
    block_count = beam_blocks.shape[0]
    slot_cap = block_count * 2 // device_total_count
    weight_rows = weights.reshape(-1, SAMP)
    tile_flat = tile_ids.reshape(-1)
    offset_flat = offsets.reshape(-1)
    owner_dev = tile_flat // tile_count
    first_pixel_index = tile_flat % tile_count * TILE_PIX + offset_flat
    foot_range = jnp.arange(FOOT, dtype=jnp.int32)
    hit_table = (
        owner_dev[:, None] == jnp.arange(device_total_count, dtype=jnp.int32)[None, :]
    ).astype(jnp.int32)
    rank_pos = jnp.sum(jnp.cumsum(hit_table, axis=0) * hit_table, axis=1) - 1
    slot_index = owner_dev * slot_cap + rank_pos
    requests = (
        jnp.full((device_total_count * slot_cap,), -1, jnp.int32)
        .at[slot_index]
        .set(first_pixel_index)
    )
    asked_start = lax.all_to_all(
        requests.reshape(device_total_count, slot_cap),
        DET_TM,
        split_axis=0,
        concat_axis=0,
        tiled=True,
    )
    pick_index = jnp.maximum(asked_start, 0)[:, :, None] + foot_range

    def adjoint_sum(back_vals):
        send_buf = (
            jnp.zeros((device_total_count * slot_cap, FOOT), jnp.float32)
            .at[slot_index]
            .set(back_vals)
        )
        got_parts = lax.all_to_all(
            send_buf.reshape(device_total_count, slot_cap, FOOT).astype(jnp.bfloat16),
            DET_TM,
            split_axis=0,
            concat_axis=0,
            tiled=True,
        ).astype(jnp.float32)
        got_parts = jnp.where(asked_start[:, :, None] >= 0, got_parts, 0.0)
        total = (
            jnp.zeros((tile_count * TILE_PIX,), jnp.float32)
            .at[pick_index.reshape(-1)]
            .add(got_parts.reshape(-1))
        )
        return total.reshape(tile_count, TILE_PIX)

    def fetch_foot(map_field):
        reply_buf = map_field.reshape(-1).astype(jnp.bfloat16)[pick_index]
        arrived = exchange_by_chip(reply_buf, (("det", "tm_0", "tm_1"), "tm_2"), (1, 0), 0, 0)
        return arrived.reshape(-1, FOOT)[slot_index]

    def prior_term(map_field):
        edge_pair = jnp.stack([map_field[:, 0], map_field[:, TILE_PIX - 1]], axis=0)
        all_edges = lax.all_gather(edge_pair, DET_TM, axis=1, tiled=True)
        left_edge = all_edges[1][neighbours[:, 0]]
        right_edge = all_edges[0][neighbours[:, 1]]
        lefts = jnp.concatenate([left_edge[:, None], map_field[:, :-1]], axis=1)
        rights = jnp.concatenate([map_field[:, 1:], right_edge[:, None]], axis=1)
        return smooth_weight * (2.0 * map_field - lefts - rights) + ridge_weight * map_field

    def project_back(weighted):
        return jnp.einsum("bsf,bs->bf", beam_blocks, weighted, preferred_element_type=jnp.float32)

    def operate(map_field):
        foot = fetch_foot(map_field)
        samples = jnp.einsum("bsf,bf->bs", beam_blocks, foot, preferred_element_type=jnp.float32)
        weighted = (weight_rows * samples).astype(jnp.bfloat16)
        return adjoint_sum(project_back(weighted)) + prior_term(map_field)

    data_weighted = (weight_rows * tod.reshape(-1, SAMP).astype(jnp.float32)).astype(jnp.bfloat16)
    right_hand_vector = adjoint_sum(project_back(data_weighted))
    solution = jnp.zeros_like(right_hand_vector)
    residual = right_hand_vector

    def paired(resid_now, image_now):
        return (
            by_axis(jnp.sum(resid_now * resid_now), DET_TM),
            by_axis(jnp.sum(resid_now * image_now), DET_TM),
        )

    image_vec = operate(residual)
    norm_now, product = paired(residual, image_vec)
    step_size = norm_now / product
    direction = residual
    along_vec = image_vec
    for iteration in range(ITERS):
        solution = solution + step_size * direction
        residual = residual - step_size * along_vec
        if iteration + 1 < ITERS:
            image_vec = operate(residual)
            norm_next, product = paired(residual, image_vec)
            ratio = norm_next / norm_now
            step_size = norm_next / (product - ratio * norm_next / step_size)
            direction = residual + ratio * direction
            along_vec = image_vec + ratio * along_vec
            norm_now = norm_next
    return (solution, residual)


def solution(mesh):
    split = Mesh(mesh.devices.reshape(mesh.shape["det"], 4, 4, 2), ("det", "tm_0", "tm_1", "tm_2"))
    in_specs = (
        P("det", TM, None),
        P("det", TM, None, None),
        P("det", TM, None),
        P("det", TM),
        P("det", TM),
        P(DET_TM, None),
    )
    out_specs = (P(DET_TM, None), P(DET_TM, None))
    return jax.shard_map(
        per_device, mesh=split, in_specs=in_specs, out_specs=out_specs, check_vma=False
    )
```

profile of v0, /device:TPU:1, one launch (start us, length us, event | category | flops | bytes accessed | tf_op | source)
XLA Modules:
  0.0 1347.0 jit_solution(14877927946325925046)
XLA Ops:
  0.6 0.8 reshape.226
  1.4 0.8 reshape.225
  2.1 0.8 reshape.227
  3.4 1.0 scatter_custom_fusion
  4.4 0.8 all_to_all.27
  5.1 11.5 all-to-all-start
  16.6 0.8 fusion.33
  17.4 0.9 fusion
  18.3 4.6 fusion.7
  22.9 0.9 scatter_custom_fusion.1
  24.5 1.4 all-to-all-done
  25.9 8.3 all-to-all-start.1
  35.3 8.3 all-to-all-done.1
  43.8 226.1 %scatter_custom_fusion.2 = f32[16384]{0:T(1024)S(1)} fusion(s32[32768]{0:T(1024)S(1)} %bitcast.131, f32[32768]{0:T(1024)S(1)} %bitcast.135, f32[]{:T(128)} %constant.20.clone.1), kind=kCustom, calls=%fused_computation.71 | custom fusion | flops 32768 | bytes 65540 | tf_op jit(solution)/shard_map/scatter-add | solution.py:99
  270.2 201.3 %gather_fusion = bf16[32768]{0:T(1024)(128)(2,1)S(1)} fusion(bf16[16384]{0:T(1024)(128)(2,1)S(1)} %convert_element_type.58, s32[32768]{0:T(1024)S(1)} %broadcast_clamp_fusion), kind=kCustom, calls=%fused_computation | custom fusion | bytes 262144 | tf_op jit(solution)/shard_map/gather | solution.py:104
  471.5 4.6 all_to_all.44
  476.1 0.7 copy.35
  476.8 4.8 all-to-all-start.3
  481.6 36.5 %all-gather = f32[128,16,2]{1,2,0:T(2,128)S(1)} all-gather(f32[1,16,2]{1,2,0:T(2,128)S(1)} %maximum_bitcast_fusion), channel_id=1, replica_groups=mesh['det'=4,'tm_0'=4,'tm_1'=4,'tm_2'=2] {'det','tm_0','tm_1','tm_2'}, dimensions={0}, use_global_device_ids=true | all-gather | bytes 16512 | tf_op jit(solution)/shard_map/all_gather | solution.py:110
  519.0 0.7 gather_fusion.2
  519.8 0.7 gather_fusion.1
  520.6 5.6 fusion.11
  526.2 4.6 fusion.5
  530.8 0.9 scatter_custom_fusion.3
  532.4 5.2 all-to-all-start.4
  537.7 9.2 all-to-all-done.4
  547.1 226.1 %scatter_custom_fusion.4 = f32[16384]{0:T(1024)S(1)} fusion(s32[32768]{0:T(1024)S(1)} %bitcast.132, f32[32768]{0:T(1024)S(1)} %bitcast.136, f32[]{:T(128)} %constant.20.clone.1), kind=kCustom, calls=%fused_computation.69 | custom fusion | flops 32768 | bytes 65540 | tf_op jit(solution)/shard_map/scatter-add | solution.py:99
  773.8 7.5 all-reduce.5
  781.3 7.7 all-reduce.3
  789.0 7.1 all-reduce.1
  796.1 9.5 all-reduce.7
  807.4 201.3 %gather_fusion.4 = bf16[32768]{0:T(1024)(128)(2,1)S(1)} fusion(bf16[16384]{0:T(1024)(128)(2,1)S(1)} %get-tuple-element.26, s32[32768]{0:T(1024)S(1)} %broadcast_clamp_fusion), kind=kCustom, calls=%fused_computation.4 | custom fusion | bytes 262144 | tf_op jit(solution)/shard_map/gather | solution.py:104
  1008.8 3.8 all_to_all.45
  1012.6 0.7 copy.40
  1013.3 4.6 all-to-all-start.6
  1017.9 36.2 %all-gather.1 = f32[128,16,2]{1,2,0:T(2,128)S(1)} all-gather(f32[1,16,2]{1,2,0:T(2,128)S(1)} %maximum_bitcast_fusion.1), channel_id=1, replica_groups=mesh['det'=4,'tm_0'=4,'tm_1'=4,'tm_2'=2] {'det','tm_0','tm_1','tm_2'}, dimensions={0}, use_global_device_ids=true | all-gather | bytes 16512 | tf_op jit(solution)/shard_map/all_gather | solution.py:110
  1055.9 0.7 gather_fusion.5
  1056.6 5.6 fusion.9
  1062.3 4.6 fusion.3
  1066.8 0.9 scatter_custom_fusion.5
  1068.4 5.2 all-to-all-start.7
  1073.7 9.2 all-to-all-done.7
  1083.1 226.1 %scatter_custom_fusion.6 = f32[16384]{0:T(1024)S(1)} fusion(s32[32768]{0:T(1024)S(1)} %bitcast.133, f32[32768]{0:T(1024)S(1)} %bitcast.134, f32[]{:T(128)} %constant.20.clone.1), kind=kCustom, calls=%fused_computation.67 | custom fusion | flops 32768 | bytes 65540 | tf_op jit(solution)/shard_map/scatter-add | solution.py:99
  1309.9 7.5 all-reduce.4
  1317.4 7.7 all-reduce.2
  1325.1 7.1 all-reduce
  1332.2 9.4 all-reduce.6
  1346.3 0.7 multiply_subtract_fusion
  (64 shorter events, 9.1 us)
Async XLA Ops:
  5.1 20.8 %all-to-all-start = ((s32[128,1,2]{2,1,0:T(1,128)}), s32[128,1,2]{2,1,0:T(1,128)S(1)}, u32[]{:S(2)}, u32[]{:S(2)}) async-start(s32[128,1,2]{2,1,0:T(1,128)} %bitcast.2), calls=%async_computation | async-start | bytes 131072 | tf_op jit(solution)/shard_map/all_to_all | solution.py:73
  25.9 17.6 %all-to-all-start.1 = ((bf16[128,2,128]{2,1,0:T(2,128)(2,1)}), bf16[128,2,128]{2,1,0:T(2,128)(2,1)S(1)}, u32[]{:S(2)}, u32[]{:S(2)}) async-start(bf16[128,2,128]{2,1,0:T(2,128)(2,1)} %bitcast.13), calls=%async_computation.1 | async-start | bytes 131072 | tf_op jit(solution)/shard_map/all_to_all | solution.py:88
  471.5 54.7 %copy-start = (f32[2,64,256]{2,1,0:T(8,128)S(1)}, f32[2,64,256]{2,1,0:T(8,128)}, u32[]{:S(2)}) copy-start(f32[2,64,256]{2,1,0:T(8,128)} %param.8) | copy-start | bytes 393220
  476.8 43.0 %all-to-all-start.3 = ((bf16[64,2,1,2,128]{4,3,1,2,0:T(2,128)(2,1)}), bf16[64,2,1,2,128]{4,3,1,2,0:T(2,128)(2,1)S(1)}, u32[]{:S(2)}, u32[]{:S(2)}) async-start(bf16[64,2,1,2,128]{4,3,1,2,0:T(2,128)(2,1)} %copy.35), calls=%async_computation.3 | async-start | bytes 131072 | tf_op jit(solution)/shard_map/all_to_all | solution.py:35
  532.4 14.5 %all-to-all-start.4 = ((bf16[128,2,128]{2,1,0:T(2,128)(2,1)}), bf16[128,2,128]{2,1,0:T(2,128)(2,1)S(1)}, u32[]{:S(2)}, u32[]{:S(2)}) async-start(bf16[128,2,128]{2,1,0:T(2,128)(2,1)} %bitcast.23), calls=%async_computation.4 | async-start | bytes 131072 | tf_op jit(solution)/shard_map/all_to_all | solution.py:88
  1013.3 42.6 %all-to-all-start.6 = ((bf16[64,2,1,2,128]{4,3,1,2,0:T(2,128)(2,1)}), bf16[64,2,1,2,128]{4,3,1,2,0:T(2,128)(2,1)S(1)}, u32[]{:S(2)}, u32[]{:S(2)}) async-start(bf16[64,2,1,2,128]{4,3,1,2,0:T(2,128)(2,1)} %copy.40), calls=%async_computation.6 | async-start | bytes 131072 | tf_op jit(solution)/shard_map/all_to_all | solution.py:35
  1068.4 14.5 %all-to-all-start.7 = ((bf16[128,2,128]{2,1,0:T(2,128)(2,1)}), bf16[128,2,128]{2,1,0:T(2,128)(2,1)S(1)}, u32[]{:S(2)}, u32[]{:S(2)}) async-start(bf16[128,2,128]{2,1,0:T(2,128)(2,1)} %bitcast.41), calls=%async_computation.7 | async-start | bytes 131072 | tf_op jit(solution)/shard_map/all_to_all | solution.py:88
where the time goes:
time: 1350 us
  other arithmetic  686 us (51%)
  local copies, waits for them, and re-layouts  416 us (31%)
  blocking collectives  145 us (11%)
  starting transfers between devices  39.6 us (3%)
  waiting for transfers between devices  28.1 us (2%)
  matrix products  25 us (2%)
    scatter-add x3, other arithmetic, adjoint_sum(): total = jnp.zeros((tile_count * TILE_PIX,), jnp.float32).at[pick_index.re...  678 us
    gather x2, local copies, waits for them, and re-layouts, fetch_foot(): reply_buf = map_field.reshape(-1).astype(jnp.bfloat16)[pick_index]  403 us
    all_gather x2, blocking collectives, prior_term(): all_edges = lax.all_gather(edge_pair, DET_TM, axis=1, tiled=True)  72.7 us
    psum x8, blocking collectives, by_axis(): x = lax.psum(x, axis)  63.6 us
  transfers between devices with their start and end apart: 6, of which 4 were waited for; matrix products, arithmetic and copies ran while one was open for 1% of the time, Pallas kernels for 0%

commit v1 on v0

v1 whole, which is shorter than its diff:
```python
import jax
import jax.numpy as jnp
from jax import lax
from jax.experimental import pallas as pl
from jax.experimental.pallas import tpu as pltpu
from jax.sharding import Mesh
from jax.sharding import PartitionSpec as P


DET_TM = ("det", "tm_0", "tm_1", "tm_2")
TM = ("tm_0", "tm_1", "tm_2")
SAMP = 256
FOOT = 128
L = 128
TILE = 16
ROW_STEP = 16
SCALARS = 64

smooth_weight = 2.0
ridge_weight = 0.5

F32 = jnp.float32
BF16 = jnp.bfloat16


def _roll(x, shift, axis):
    return pltpu.roll(x, shift, axis)


def _iota(shape, dim):
    return lax.broadcasted_iota(jnp.int32, shape, dim)


def _dot(a, b):
    return jnp.dot(a, b, preferred_element_type=F32)


def _dot_nt(a, b):
    return lax.dot_general(a, b, (((1,), (1,)), ((), ())), preferred_element_type=F32)


def _onehot(mask):
    return jnp.where(mask, 1.0, 0.0).astype(BF16)


def _to_col(row):
    eye = _iota((L, L), 0) == _iota((L, L), 1)
    return jnp.sum(jnp.where(eye, row, 0.0), axis=1, keepdims=True)


def _to_row(col):
    eye = _iota((L, L), 0) == _iota((L, L), 1)
    return jnp.sum(jnp.where(eye, col, 0.0), axis=0, keepdims=True)


def _rotate(x, amount):
    for bit in range(7):
        x = jnp.where((amount & (1 << bit)) != 0, _roll(x, 1 << bit, 1), x)
    return x


def _as_row(ids, scratch):
    scratch[...] = jnp.zeros(scratch.shape, F32)
    scratch[0:2, 0:64] = ids.astype(F32)
    x = scratch[...]
    return x[0:1] + _roll(x, 64, 1)[1:2]


def _pieces(value, first):
    hi = value.astype(BF16).astype(F32)
    mid = (value - hi).astype(BF16).astype(F32)
    lo = value - hi - mid
    lane = _iota((1, L), 1)
    return jnp.where(
        lane == first, hi, jnp.where(lane == first + 1, mid, jnp.where(lane == first + 2, lo, 0.0))
    )


def _whole(row, first):
    lane = _iota((1, L), 1)
    return jnp.sum(
        jnp.where((lane >= first) & (lane < first + 3), row, 0.0), axis=1, keepdims=True
    )


def _total(x):
    return jnp.sum(jnp.sum(x, axis=0, keepdims=True), axis=1, keepdims=True)


def _blocks_of(owner_row, j):
    block = _iota((L, L), 1)
    return _onehot((_iota((L, L), 0) == owner_row) & ((block & 1) == j))


def first_message(tile_row, offset_row, back):
    tile = tile_row.astype(jnp.int32)
    offset = offset_row.astype(jnp.int32)
    owner = tile >> 4
    start_row = (offset >> 7) * ROW_STEP + (tile & 15)
    shift = offset & 127
    shift_col = _to_col(shift.astype(F32)).astype(jnp.int32)
    turned = _rotate(back, shift_col).astype(BF16)
    to_0 = _blocks_of(owner, 0)
    to_1 = _blocks_of(owner, 1)
    line = _iota((L, L), 0)
    place = 2 * (_iota((L, L), 1) & 1)
    facts = jnp.where(
        line == place,
        start_row.astype(F32),
        jnp.where(line == place + 1, shift.astype(F32), 0.0),
    ).astype(BF16)
    return (
        _dot(to_0, turned).astype(BF16),
        _dot(to_1, turned).astype(BF16),
        _dot_nt(to_0 + to_1, facts).astype(BF16),
    )


def block_tables(tile_row, offset_row):
    owner = tile_row.astype(jnp.int32) >> 4
    shift = offset_row.astype(jnp.int32) & 127
    owner_col = _to_col(owner.astype(F32)).astype(jnp.int32)
    shift_col = _to_col(shift.astype(F32)).astype(jnp.int32)
    block = _iota((L, L), 0)
    device = _iota((L, L), 1)
    get = [_onehot((device == owner_col) & ((block & 1) == j)) for j in range(2)]
    put = [_blocks_of(owner, j) for j in range(2)]
    return get, put, jnp.broadcast_to(shift_col, (L, L))


def owner_tables(facts):
    facts = facts.astype(F32)
    pick, place, shifts = [], [], []
    for j in range(2):
        start_col = facts[:, 2 * j : 2 * j + 1]
        start_row = _to_row(start_col)
        for step in (0, ROW_STEP):
            pick.append(_onehot(_iota((L, L), 1).astype(F32) == start_col + step))
            place.append(_onehot(_iota((L, L), 0).astype(F32) == start_row + step))
        shifts.append(jnp.broadcast_to(facts[:, 2 * j + 1 : 2 * j + 2], (L, L)).astype(jnp.int32))
    return pick, place, shifts


def add_up(got, place, shifts):
    lane = _iota((L, L), 1)
    total = None
    for j in range(2):
        x = got[j].astype(F32)
        upper = jnp.where(lane >= shifts[j], x, 0.0).astype(BF16)
        lower = jnp.where(lane < shifts[j], x, 0.0).astype(BF16)
        part = _dot(place[2 * j], upper) + _dot(place[2 * j + 1], lower)
        total = part if total is None else total + part
    return total


def reply(field, pick, shifts):
    lane = _iota((L, L), 1)
    field = field.astype(BF16)
    return [
        jnp.where(
            lane >= shifts[j], _dot(pick[2 * j], field), _dot(pick[2 * j + 1], field)
        ).astype(BF16)
        for j in range(2)
    ]


def edge_row(field):
    lane = _iota((TILE, L), 1)
    tile = _iota((TILE, L), 0)
    first = field[0:TILE, 0:1]
    last = field[L - TILE : L, L - 1 : L]
    out = jnp.zeros((TILE, L), F32)
    for k, value in enumerate((first, last)):
        hi = value.astype(BF16).astype(F32)
        out = out + jnp.where(lane == tile + 32 * k, hi, 0.0)
        out = out + jnp.where(lane == tile + 32 * k + 16, value - hi, 0.0)
    return jnp.sum(out, axis=0, keepdims=True)


def outer_edges(edges, neighbours):
    lane = _iota((TILE, L), 1)
    found = []
    for side, base in ((0, 32), (1, 0)):
        tile = neighbours[:, side : side + 1]
        rows = _dot(_onehot(lane == (tile >> 4)), edges)
        at = base + (tile & 15)
        found.append(
            jnp.sum(jnp.where((lane == at) | (lane == at + 16), rows, 0.0), axis=1, keepdims=True)
        )
    return found


def prior(field, before, after):
    lane = _iota((L, L), 1)
    row = _iota((L, L), 0)
    to_right = _roll(field, 1, 1)
    to_left = _roll(field, L - 1, 1)
    left_in = _roll(to_right, ROW_STEP, 0)
    right_in = _roll(to_left, L - ROW_STEP, 0)
    pad = jnp.zeros((L - TILE, 1), F32)
    left_in = jnp.where(row < TILE, jnp.concatenate([before, pad], axis=0), left_in)
    right_in = jnp.where(row >= L - TILE, jnp.concatenate([pad, after], axis=0), right_in)
    lefts = jnp.where(lane == 0, left_in, to_right)
    rights = jnp.where(lane == L - 1, right_in, to_left)
    return smooth_weight * (2.0 * field - lefts - rights) + ridge_weight * field


def take_reply(got, get, shift):
    turned = _dot(get[0], got[0]) + _dot(get[1], got[1])
    return _rotate(turned, (L - shift) & 127)


def send_back(back, put, shift):
    turned = _rotate(back, shift).astype(BF16)
    return [_dot(put[j], turned).astype(BF16) for j in range(2)]


def pair_rows(foot):
    row = _iota((L, L), 0)
    left = jnp.where(row < L // 2, foot, 0.0).astype(BF16)
    right = jnp.where(row >= L // 2, foot, 0.0).astype(BF16)
    return jnp.concatenate([left, right], axis=1)


RHS_STEP = 16
NORMAL_STEP = 8
APPLY_STEP = 16


def rhs_kernel(tile_ref, offset_ref, tod_ref, weight_ref, beam_ref, message_ref, back, scratch):
    g = pl.program_id(0)
    weighted = (weight_ref[...] * tod_ref[...].astype(F32)).astype(BF16)
    row = _iota((RHS_STEP, FOOT), 0)
    out = jnp.zeros((RHS_STEP, FOOT), F32)
    for k in range(RHS_STEP):
        out = jnp.where(row == k, _dot(weighted, beam_ref[k]), out)
    back[pl.ds(pl.multiple_of(g * RHS_STEP, RHS_STEP), RHS_STEP), :] = out

    @pl.when(g == pl.num_programs(0) - 1)
    def _():
        tile_row = _as_row(tile_ref[...], scratch)
        offset_row = _as_row(offset_ref[...], scratch)
        parts = first_message(tile_row, offset_row, back[...])
        for k in range(3):
            message_ref[k] = parts[k]


def normal_kernel(tile_ref, offset_ref, weight_ref, beam_ref, normal_ref, get_ref, put_ref, shift_ref, scratch):
    for k in range(NORMAL_STEP):
        for det in range(2):
            beam = beam_ref[det, k]
            turned = beam.astype(F32).T * weight_ref[det, k : k + 1, :]
            normal_ref[k, :, det * FOOT : (det + 1) * FOOT] = _dot(turned.astype(BF16), beam).astype(BF16)

    @pl.when(pl.program_id(0) == 0)
    def _():
        tile_row = _as_row(tile_ref[...], scratch)
        offset_row = _as_row(offset_ref[...], scratch)
        get, put, shift = block_tables(tile_row, offset_row)
        for j in range(2):
            get_ref[j] = get[j]
            put_ref[j] = put[j]
        shift_ref[...] = shift


def start_kernel(got_ref, field_ref, message_ref, pick_ref, place_ref, shift_ref):
    pick, place, shifts = owner_tables(got_ref[2])
    field = add_up((got_ref[0], got_ref[1]), place, shifts)
    replies = reply(field, pick, shifts)
    field_ref[...] = field
    message_ref[0] = replies[0]
    message_ref[1] = replies[1]
    message_ref[2] = jnp.broadcast_to(edge_row(field), (L, L)).astype(BF16)
    for k in range(4):
        pick_ref[k] = pick[k]
        place_ref[k] = place[k]
    for j in range(2):
        shift_ref[j] = shifts[j]


def apply_step(normal_ref, pairs, back):
    g = pl.program_id(0)
    lane = _iota((L, L), 1) & 63
    out = _dot_nt(normal_ref[...].reshape(APPLY_STEP * L, 2 * L), pairs[...])
    acc = back[...]
    for k in range(APPLY_STEP):
        acc = jnp.where(lane == g * APPLY_STEP + k, out[k * L : (k + 1) * L], acc)
    back[...] = acc


def first_apply_kernel(got_ref, get_ref, put_ref, shift_ref, normal_ref, message_ref, foot_ref, pairs, back):
    g = pl.program_id(0)

    @pl.when(g == 0)
    def _():
        foot = take_reply((got_ref[0], got_ref[1]), (get_ref[0], get_ref[1]), shift_ref[...])
        foot_ref[...] = foot
        pairs[...] = pair_rows(foot)
        back[...] = jnp.zeros((L, L), F32)

    apply_step(normal_ref, pairs, back)

    @pl.when(g == pl.num_programs(0) - 1)
    def _():
        parts = send_back(back[...].T, (put_ref[0], put_ref[1]), shift_ref[...])
        message_ref[0] = parts[0]
        message_ref[1] = parts[1]


def middle_kernel(got_ref, before_ref, field_ref, neighbour_ref, pick_ref, place_ref, shift_ref, image_ref, prior_ref, message_ref):
    field = field_ref[...]
    pick = [pick_ref[k] for k in range(4)]
    place = [place_ref[k] for k in range(4)]
    shifts = [shift_ref[j] for j in range(2)]
    before, after = outer_edges(before_ref[2], neighbour_ref[...])
    smooth = prior(field, before, after)
    image = add_up((got_ref[0], got_ref[1]), place, shifts) + smooth
    replies = reply(image, pick, shifts)
    prior_ref[...] = smooth
    image_ref[...] = image
    message_ref[0] = replies[0]
    message_ref[1] = replies[1]
    extra = (
        edge_row(image)
        + _pieces(_total(field * field), SCALARS)
        + _pieces(_total(field * image), SCALARS + 3)
    )
    message_ref[2] = jnp.broadcast_to(extra, (L, L)).astype(BF16)


def second_apply_kernel(
    got_ref, get_ref, put_ref, shift_ref, normal_ref, foot_ref, field_ref, image_ref, smooth_ref, neighbour_ref,
    message_ref, residual_ref, prior_ref, sums_ref, pairs, back, foot_scr,
):
    g = pl.program_id(0)

    @pl.when(g == 0)
    def _():
        sums = jnp.sum(got_ref[2].astype(F32), axis=0, keepdims=True)
        sums_ref[...] = sums
        step = _whole(sums, SCALARS) / _whole(sums, SCALARS + 3)
        taken = take_reply((got_ref[0], got_ref[1]), (get_ref[0], get_ref[1]), shift_ref[...])
        foot = (foot_ref[...] - step * taken).astype(BF16).astype(F32)
        foot_scr[...] = foot
        pairs[...] = pair_rows(foot)
        back[...] = jnp.zeros((L, L), F32)
        image = image_ref[...]
        before, after = outer_edges(got_ref[2], neighbour_ref[...])
        residual_ref[...] = field_ref[...] - step * image
        prior_ref[...] = smooth_ref[...] - step * prior(image, before, after)

    apply_step(normal_ref, pairs, back)

    @pl.when(g == pl.num_programs(0) - 1)
    def _():
        turned = back[...].T
        parts = send_back(turned, (put_ref[0], put_ref[1]), shift_ref[...])
        message_ref[0] = parts[0]
        message_ref[1] = parts[1]
        residual = residual_ref[...]
        square = _total(residual * residual)
        product = _total(foot_scr[...] * turned + residual * prior_ref[...])
        extra = _pieces(square, SCALARS) + _pieces(product, SCALARS + 3)
        message_ref[2] = jnp.broadcast_to(extra, (L, L)).astype(BF16)


def last_kernel(got_ref, place_ref, shift_ref, field_ref, image_ref, residual_ref, smooth_ref, sums_ref, solution_ref, rest_ref):
    place = [place_ref[k] for k in range(4)]
    shifts = [shift_ref[j] for j in range(2)]
    residual = residual_ref[...]
    field = field_ref[...]
    image = add_up((got_ref[0], got_ref[1]), place, shifts) + smooth_ref[...]
    sums = sums_ref[...]
    more = jnp.sum(got_ref[2].astype(F32), axis=0, keepdims=True)
    norm_first = _whole(sums, SCALARS)
    step_first = norm_first / _whole(sums, SCALARS + 3)
    norm = _whole(more, SCALARS)
    ratio = norm / norm_first
    step = norm / (_whole(more, SCALARS + 3) - ratio * norm / step_first)
    solution = step_first * field + step * (residual + ratio * field)
    rest = residual - step * (image + ratio * image_ref[...])
    for q in range(8):
        solution_ref[:, q * L : (q + 1) * L] = solution[q * TILE : (q + 1) * TILE]
        rest_ref[:, q * L : (q + 1) * L] = rest[q * TILE : (q + 1) * TILE]


def _shape(shape, dtype):
    return jax.ShapeDtypeStruct(shape, dtype)


def _full(shape):
    return pl.BlockSpec(shape, lambda g: (0,) * len(shape))


MAP = (L, L)
WIDE = _shape(MAP, F32)


def call(kernel, grid, in_specs, outs, out_specs, scratch, args, flops, size):
    return pl.pallas_call(
        kernel,
        grid=(grid,),
        in_specs=in_specs,
        out_specs=out_specs,
        out_shape=outs,
        scratch_shapes=scratch,
        compiler_params=pltpu.CompilerParams(
            dimension_semantics=("arbitrary",), vmem_limit_bytes=40 * 2**20
        ),
        cost_estimate=pl.CostEstimate(flops=flops, bytes_accessed=size, transcendentals=0),
    )(*args)


def whole_call(kernel, outs, args, scratch=()):
    return call(
        kernel, 1, [_full(a.shape) for a in args], outs, [_full(o.shape) for o in outs], scratch, args, 2**25, 2**19
    )


def exchange(x):
    return lax.all_to_all(x, DET_TM, split_axis=1, concat_axis=1, tiled=True)


def per_device(tod, pointing, weights, tile_ids, offsets, neighbours):
    ids = [_full(tile_ids.shape)] * 2
    half = L // 2

    (message,) = call(
        rhs_kernel,
        L // RHS_STEP,
        ids
        + [
            pl.BlockSpec((RHS_STEP, SAMP), lambda g: (g, 0)),
            pl.BlockSpec((RHS_STEP, SAMP), lambda g: (g, 0)),
            pl.BlockSpec((RHS_STEP, SAMP, FOOT), lambda g: (g, 0, 0)),
        ],
        [_shape((3, L, L), BF16)],
        [_full((3, L, L))],
        [pltpu.VMEM((L, FOOT), F32), pltpu.VMEM((8, L), F32)],
        (
            tile_ids,
            offsets,
            tod.reshape(L, SAMP),
            weights.reshape(L, SAMP),
            pointing.reshape(L, SAMP, FOOT),
        ),
        2**24,
        2**23,
    )
    got = exchange(message)

    normal, get, put, shift = call(
        normal_kernel,
        half // NORMAL_STEP,
        ids
        + [
            pl.BlockSpec((2, NORMAL_STEP, SAMP), lambda g: (0, g, 0)),
            pl.BlockSpec((2, NORMAL_STEP, SAMP, FOOT), lambda g: (0, g, 0, 0)),
        ],
        [
            _shape((half, FOOT, 2 * FOOT), BF16),
            _shape((2, L, L), BF16),
            _shape((2, L, L), BF16),
            _shape((L, L), jnp.int32),
        ],
        [
            pl.BlockSpec((NORMAL_STEP, FOOT, 2 * FOOT), lambda g: (g, 0, 0)),
            _full((2, L, L)),
            _full((2, L, L)),
            _full((L, L)),
        ],
        [pltpu.VMEM((8, L), F32)],
        (tile_ids, offsets, weights, pointing),
        2**30,
        12 * 2**20,
    )

    field, message, pick, place, shifts = whole_call(
        start_kernel,
        [WIDE, _shape((3, L, L), BF16), _shape((4, L, L), BF16), _shape((4, L, L), BF16), _shape((2, L, L), jnp.int32)],
        (got,),
    )
    got_first = exchange(message)

    normal_spec = pl.BlockSpec((APPLY_STEP, FOOT, 2 * FOOT), lambda g: (g, 0, 0))
    table_specs = [_full((2, L, L)), _full((2, L, L)), _full((L, L)), normal_spec]
    message, foot = call(
        first_apply_kernel,
        half // APPLY_STEP,
        [_full((3, L, L))] + table_specs,
        [_shape((2, L, L), BF16), WIDE],
        [_full((2, L, L)), _full(MAP)],
        [pltpu.VMEM((L, 2 * L), BF16), pltpu.VMEM(MAP, F32)],
        (got_first, get, put, shift, normal),
        2**29,
        2**22,
    )
    got = exchange(message)

    image, smooth, message = whole_call(
        middle_kernel,
        [WIDE, WIDE, _shape((3, L, L), BF16)],
        (got, got_first, field, neighbours, pick, place, shifts),
    )
    got = exchange(message)

    message, residual, smooth, sums = call(
        second_apply_kernel,
        half // APPLY_STEP,
        [_full((3, L, L))] + table_specs + [_full(MAP)] * 4 + [_full(neighbours.shape)],
        [_shape((3, L, L), BF16), WIDE, WIDE, _shape((1, L), F32)],
        [_full((3, L, L)), _full(MAP), _full(MAP), _full((1, L))],
        [pltpu.VMEM((L, 2 * L), BF16), pltpu.VMEM(MAP, F32), pltpu.VMEM(MAP, F32)],
        (got, get, put, shift, normal, foot, field, image, smooth, neighbours),
        2**29,
        2**22,
    )
    got = exchange(message)

    return tuple(
        whole_call(
            last_kernel,
            [_shape((TILE, 8 * L), F32)] * 2,
            (got, place, shifts, field, image, residual, smooth, sums),
        )
    )


def solution(mesh):
    split = Mesh(mesh.devices.reshape(mesh.shape["det"], 4, 4, 2), DET_TM)
    in_specs = (
        P("det", TM, None),
        P("det", TM, None, None),
        P("det", TM, None),
        P("det", TM),
        P("det", TM),
        P(DET_TM, None),
    )
    out_specs = (P(DET_TM, None), P(DET_TM, None))
    return jax.shard_map(
        per_device, mesh=split, in_specs=in_specs, out_specs=out_specs, check_vma=False
    )
```

time: 1350 us -> 109 us (0.08)
  other arithmetic: 686 us -> 0 us
  local copies, waits for them, and re-layouts: 416 us -> 18 us
  blocking collectives: 145 us -> 50.1 us
  starting transfers between devices: 39.6 us -> 14.3 us
  matrix products: 25 us -> 0 us
  waiting for transfers between devices: 28.1 us -> 9.19 us
  Pallas kernels: 0 us -> 16.5 us
    scatter-add x3 -> x0, other arithmetic: 678 us -> none  [adjoint_sum(): total = jnp.zeros((tile_count * TILE_PIX,), jnp.float32).at[pick_index.re...]
    gather x8 -> x0, local copies, waits for them, and re-layouts: 407 us -> none  [the longest x2 403 us: fetch_foot(): reply_buf = map_field.reshape(-1).astype(jnp.bfloat16)[pick_index]]
    all_gather x2 -> x0, blocking collectives: 72.7 us -> none  [prior_term(): all_edges = lax.all_gather(edge_pair, DET_TM, axis=1, tiled=True)]
    psum x8 -> x0, blocking collectives: 63.6 us -> none  [by_axis(): x = lax.psum(x, axis)]
    all_to_all x2 -> x3, blocking collectives: 8.38 us -> 50.1 us  [exchange(): return lax.all_to_all(x, DET_TM, split_axis=1, concat_axis=1, tiled=True)]
    all_to_all x6 -> x2, starting transfers between devices: 39.6 us -> 14.3 us  [exchange(): return lax.all_to_all(x, DET_TM, split_axis=1, concat_axis=1, tiled=True)]
    dot_general x5 -> x0, matrix products: 25 us -> none  [the longest x3 13.7 us: project_back(): jnp.einsum('bsf,bs->bf', beam_blocks, weighted, preferred_element_type=jn...]
    all_to_all x6 -> x2, waiting for transfers between devices: 28.1 us -> 9.19 us  [exchange(): return lax.all_to_all(x, DET_TM, split_axis=1, concat_axis=1, tiled=True)]
  transfers between devices with their start and end apart: 6 -> 2, of which waited for: 4 -> 1; matrix products, arithmetic and copies ran while one was open for 1% -> 0% of each run, Pallas kernels for 0% -> 5%
where the time goes in v1:
time: 109 us
  blocking collectives  50.1 us (46%)
  local copies, waits for them, and re-layouts  18 us (17%)
  Pallas kernels  16.5 us (15%)
  starting transfers between devices  14.3 us (13%)
  waiting for transfers between devices  9.19 us (8%)
    all_to_all x3, blocking collectives, exchange(): return lax.all_to_all(x, DET_TM, split_axis=1, concat_axis=1, tiled=True)  50.1 us
    pallas_call x7, Pallas kernels, call(): pl.pallas_call(kernel, grid=(grid,), in_specs=in_specs, out_specs=out_spe...  16.5 us
    unnamed x27, local copies, waits for them, and re-layouts  16.3 us
    all_to_all x2, starting transfers between devices, exchange(): return lax.all_to_all(x, DET_TM, split_axis=1, concat_axis=1, tiled=True)  14.3 us
    all_to_all x2, waiting for transfers between devices, exchange(): return lax.all_to_all(x, DET_TM, split_axis=1, concat_axis=1, tiled=True)  9.19 us
  transfers between devices with their start and end apart: 2, of which 1 were waited for; matrix products, arithmetic and copies ran while one was open for 0% of the time, Pallas kernels for 5%

profile of v1, /device:TPU:1, one launch (start us, length us, event | category | flops | bytes accessed | tf_op | source)
XLA Modules:
  0.0 108.9 jit_solution(14414774278340751368)
XLA Ops:
  0.6 0.0 copy-start.11
  0.6 0.0 copy-start.9
  0.7 0.0 copy-start
  0.7 3.4 %copy-done = bf16[2,64,256,128]{3,2,1,0:T(8,128)(2,1)S(1)} copy-done((bf16[2,64,256,128]{3,2,1,0:T(8,128)(2,1)S(1)}, bf16[2,64,256,128]{3,2,1,0:T(8,128)(2,1)}, u32[]{:S(2)}) %copy-start) | copy-done | bytes 8388632
  4.0 0.0 copy-start.5
  4.0 0.9 copy-done.5
  4.9 0.0 copy-start.7
  5.0 0.8 copy-done.7
  5.8 0.0 copy-start.8
  5.8 0.7 copy-done.8
  6.5 0.0 copy-start.10
  6.5 0.7 copy-done.10
  7.1 0.0 copy-start.6
  7.2 2.8 %shard_map.77 = bf16[3,128,128]{2,1,0:T(8,128)(2,1)S(1)} custom-call(s32[2,64]{1,0:T(2,128)S(1)} %copy-done.8, s32[2,64]{1,0:T(2,128)S(1)} %copy-done.10, bf16[128,256]{1,0:T(8,128)(2,1)S(1)} %bitcast.5, f32[128,256]{1,0:T(8,128)S(1)} %bitcast.4, bf16[128,256,128]{2,1,0:T(8,128)(2,1)S(1)} %bitcast.3), custom_call_target="tpu_custom_call" | custom-call | flops 16777216 | bytes 8388608 | tf_op jit(solution)/shard_map/pallas_call | solution.py:400
  10.0 0.0 copy-start.12
  10.0 0.1 copy.10
  10.1 21.3 %all_to_all.25 = bf16[3,128,128]{2,0,1:T(4,128)(2,1)S(1)} all-to-all(bf16[3,128,128]{2,0,1:T(4,128)(2,1)S(1)} %copy.10), channel_id=1, replica_groups=mesh['det'=4,'tm_0'=4,'tm_1'=4,'tm_2'=2] {'det','tm_0','tm_1','tm_2'}, dimensions={1} | all-to-all | bytes 196608 | tf_op jit(solution)/shard_map/all_to_all | solution.py:421
  31.4 0.5 shard_map.78
  31.9 0.7 copy.12
  32.6 4.5 %all-to-all-start.1 = ((bf16[3,128,128]{2,0,1:T(4,128)(2,1)}), bf16[3,128,128]{2,0,1:T(4,128)(2,1)S(1)}, u32[]{:S(2)}, u32[]{:S(2)}) async-start(bf16[3,128,128]{2,0,1:T(4,128)(2,1)} %copy.12), calls=%async_computation.1 | async-start | bytes 262144 | tf_op jit(solution)/shard_map/all_to_all | solution.py:421
  37.1 0.0 copy-done.11
  37.1 0.0 copy-done.9
  37.1 0.0 copy-done.6
  37.1 0.0 copy-start.1
  37.2 3.4 %copy-done.1 = bf16[2,64,256,128]{3,2,1,0:T(8,128)(2,1)S(1)} copy-done((bf16[2,64,256,128]{3,2,1,0:T(8,128)(2,1)S(1)}, bf16[2,64,256,128]{3,2,1,0:T(8,128)(2,1)}, u32[]{:S(2)}) %copy-start.1) | copy-done | bytes 8388632
  40.5 5.4 %shard_map.79 = (bf16[64,128,256]{2,1,0:T(8,128)(2,1)S(1)}, bf16[2,128,128]{2,1,0:T(8,128)(2,1)S(1)}, bf16[2,128,128]{2,1,0:T(8,128)(2,1)S(1)}, s32[128,128]{1,0:T(8,128)S(1)}) custom-call(s32[2,64]{1,0:T(2,128)S(1)} %copy-done.9, s32[2,64]{1,0:T(2,128)S(1)} %copy-done.11, f32[2,64,256]{2,1,0:T(8,128)S(1)} %copy-done.6, bf16[2,64,256,128]{3,2,1,0:T(8,128)(2,1)S(1)} %copy-done.1), custom_call_target="tpu_custom_call" | custom-call | flops 1073741824 | bytes 12582912 | tf_op jit(solution)/shard_map/pallas_call | solution.py:400
  45.9 0.0 copy-start.2
  46.0 1.9 %copy-done.2 = bf16[64,128,256]{2,1,0:T(8,128)(2,1)} copy-done((bf16[64,128,256]{2,1,0:T(8,128)(2,1)}, bf16[64,128,256]{2,1,0:T(8,128)(2,1)S(1)}, u32[]{:S(2)}) %copy-start.2) | copy-done | bytes 4194328
  47.9 0.0 all-to-all-done.1
  47.9 0.0 copy-start.3
  47.9 2.2 %copy-done.3 = bf16[64,128,256]{2,1,0:T(8,128)(2,1)S(1)} copy-done((bf16[64,128,256]{2,1,0:T(8,128)(2,1)S(1)}, bf16[64,128,256]{2,1,0:T(8,128)(2,1)}, u32[]{:S(2)}) %copy-start.3) | copy-done | bytes 4194328
  50.1 3.1 %shard_map.80 = (bf16[2,128,128]{2,1,0:T(8,128)(2,1)S(1)}, f32[128,128]{1,0:T(8,128)S(1)}) custom-call(bf16[3,128,128]{2,1,0:T(8,128)(2,1)S(1)} %copy.13.got_ref.before_ref, bf16[2,128,128]{2,1,0:T(8,128)(2,1)S(1)} %get-tuple-element.21.get_ref, bf16[2,128,128]{2,1,0:T(8,128)(2,1)S(1)} %get-tuple-element.22.put_ref, ...), custom_call_target="tpu_custom_call" | custom-call | flops 536870912 | bytes 4194304 | tf_op jit(solution)/shard_map/pallas_call | solution.py:400
  53.2 0.7 copy.14
  53.9 9.8 %all-to-all-start.2 = ((bf16[2,128,128]{2,0,1:T(2,128)(2,1)}), bf16[2,128,128]{2,0,1:T(2,128)(2,1)S(1)}, u32[]{:S(2)}, u32[]{:S(2)}) async-start(bf16[2,128,128]{2,0,1:T(2,128)(2,1)} %copy.14), calls=%async_computation.2 | async-start | bytes 131072 | tf_op jit(solution)/shard_map/all_to_all | solution.py:421
  63.7 0.0 copy-done.12
  63.7 0.1 copy.17.neighbour_ref
  63.8 9.2 %all-to-all-done.2 = bf16[2,128,128]{2,0,1:T(2,128)(2,1)S(1)} async-done(((bf16[2,128,128]{2,0,1:T(2,128)(2,1)}), bf16[2,128,128]{2,0,1:T(2,128)(2,1)S(1)}, u32[]{:S(2)}, u32[]{:S(2)}) %all-to-all-start.2) | async-done | bytes 65568 | tf_op jit(solution)/shard_map/all_to_all | solution.py:421
  73.0 0.6 shard_map.81
  73.6 0.1 copy.18
  73.7 14.5 %all_to_all.26 = bf16[3,128,128]{2,0,1:T(4,128)(2,1)S(1)} all-to-all(bf16[3,128,128]{2,0,1:T(4,128)(2,1)S(1)} %copy.18), channel_id=1, replica_groups=mesh['det'=4,'tm_0'=4,'tm_1'=4,'tm_2'=2] {'det','tm_0','tm_1','tm_2'}, dimensions={1} | all-to-all | bytes 196608 | tf_op jit(solution)/shard_map/all_to_all | solution.py:421
  88.3 0.0 copy-start.4
  88.3 2.2 %copy-done.4 = bf16[64,128,256]{2,1,0:T(8,128)(2,1)S(1)} copy-done((bf16[64,128,256]{2,1,0:T(8,128)(2,1)S(1)}, bf16[64,128,256]{2,1,0:T(8,128)(2,1)}, u32[]{:S(2)}) %copy-start.4) | copy-done | bytes 4194328
  90.4 3.3 %shard_map.82 = (bf16[3,128,128]{2,1,0:T(8,128)(2,1)S(1)}, f32[128,128]{1,0:T(8,128)S(1)}, f32[128,128]{1,0:T(8,128)S(1)}, f32[1,128]{1,0:T(1,128)S(1)}) custom-call(bf16[3,128,128]{2,1,0:T(8,128)(2,1)S(1)} %copy.19.got_ref, bf16[2,128,128]{2,1,0:T(8,128)(2,1)S(1)} %get-tuple-element.21.get_ref, bf16[2,128,128]{2,1,0:T(8,128)(2,1)S(1)} %get-tuple-element.22.put_ref, ...), custom_call_target="tpu_custom_call" | custom-call | flops 536870912 | bytes 4194304 | tf_op jit(solution)/shard_map/pallas_call | solution.py:400
  93.7 0.1 copy.21
  93.8 14.3 %all_to_all.27 = bf16[3,128,128]{2,0,1:T(4,128)(2,1)S(1)} all-to-all(bf16[3,128,128]{2,0,1:T(4,128)(2,1)S(1)} %copy.21), channel_id=1, replica_groups=mesh['det'=4,'tm_0'=4,'tm_1'=4,'tm_2'=2] {'det','tm_0','tm_1','tm_2'}, dimensions={1} | all-to-all | bytes 196608 | tf_op jit(solution)/shard_map/all_to_all | solution.py:421
  108.1 0.8 shard_map.83
  (5 shorter events, 0.1 us)
Async XLA Ops:
  0.6 36.5 %copy-start.11 = (s32[2,64]{1,0:T(2,128)S(1)}, s32[2,64]{1,0:T(2,128)}, u32[]{:S(2)}) copy-start(s32[2,64]{1,0:T(2,128)} %offset_ref.3) | copy-start | bytes 1540
  0.6 36.5 %copy-start.9 = (s32[2,64]{1,0:T(2,128)S(1)}, s32[2,64]{1,0:T(2,128)}, u32[]{:S(2)}) copy-start(s32[2,64]{1,0:T(2,128)} %tile_ref.3) | copy-start | bytes 1540
  0.7 3.4 %copy-start = (bf16[2,64,256,128]{3,2,1,0:T(8,128)(2,1)S(1)}, bf16[2,64,256,128]{3,2,1,0:T(8,128)(2,1)}, u32[]{:S(2)}) copy-start(bf16[2,64,256,128]{3,2,1,0:T(8,128)(2,1)} %beam_ref.1) | copy-start | bytes 25165828
  4.0 0.9 copy-start.5
  4.9 0.8 copy-start.7
  5.8 0.7 copy-start.8
  6.5 0.7 copy-start.10
  7.1 30.0 %copy-start.6 = (f32[2,64,256]{2,1,0:T(8,128)S(1)}, f32[2,64,256]{2,1,0:T(8,128)}, u32[]{:S(2)}) copy-start(f32[2,64,256]{2,1,0:T(8,128)} %weight_ref.1) | copy-start | bytes 393220
  10.0 53.7 %copy-start.12 = (s32[16,2]{0,1:T(2,128)S(1)}, s32[16,2]{0,1:T(2,128)}, u32[]{:S(2)}) copy-start(s32[16,2]{0,1:T(2,128)} %param.11) | copy-start | bytes 388
  32.6 15.3 %all-to-all-start.1 = ((bf16[3,128,128]{2,0,1:T(4,128)(2,1)}), bf16[3,128,128]{2,0,1:T(4,128)(2,1)S(1)}, u32[]{:S(2)}, u32[]{:S(2)}) async-start(bf16[3,128,128]{2,0,1:T(4,128)(2,1)} %copy.12), calls=%async_computation.1 | async-start | bytes 262144 | tf_op jit(solution)/shard_map/all_to_all | solution.py:421
  37.1 3.4 %copy-start.1 = (bf16[2,64,256,128]{3,2,1,0:T(8,128)(2,1)S(1)}, bf16[2,64,256,128]{3,2,1,0:T(8,128)(2,1)}, u32[]{:S(2)}) copy-start(bf16[2,64,256,128]{3,2,1,0:T(8,128)(2,1)} %beam_ref.1) | copy-start | bytes 25165828
  45.9 1.9 %copy-start.2 = (bf16[64,128,256]{2,1,0:T(8,128)(2,1)}, bf16[64,128,256]{2,1,0:T(8,128)(2,1)S(1)}, u32[]{:S(2)}) copy-start(bf16[64,128,256]{2,1,0:T(8,128)(2,1)S(1)} %get-tuple-element.24.normal_ref) | copy-start | bytes 12582916
  47.9 2.2 %copy-start.3 = (bf16[64,128,256]{2,1,0:T(8,128)(2,1)S(1)}, bf16[64,128,256]{2,1,0:T(8,128)(2,1)}, u32[]{:S(2)}) copy-start(bf16[64,128,256]{2,1,0:T(8,128)(2,1)} %copy-done.2) | copy-start | bytes 12582916
  53.9 19.1 %all-to-all-start.2 = ((bf16[2,128,128]{2,0,1:T(2,128)(2,1)}), bf16[2,128,128]{2,0,1:T(2,128)(2,1)S(1)}, u32[]{:S(2)}, u32[]{:S(2)}) async-start(bf16[2,128,128]{2,0,1:T(2,128)(2,1)} %copy.14), calls=%async_computation.2 | async-start | bytes 131072 | tf_op jit(solution)/shard_map/all_to_all | solution.py:421
  88.3 2.2 %copy-start.4 = (bf16[64,128,256]{2,1,0:T(8,128)(2,1)S(1)}, bf16[64,128,256]{2,1,0:T(8,128)(2,1)}, u32[]{:S(2)}) copy-start(bf16[64,128,256]{2,1,0:T(8,128)(2,1)} %copy-done.2) | copy-start | bytes 12582916

commit v2 on v1

--- a/solution.py
+++ b/solution.py
@@ -181,7 +181,9 @@
     lane = _iota((TILE, L), 1)
     found = []
     for side, base in ((0, 32), (1, 0)):
-        tile = neighbours[:, side : side + 1]
+        line = neighbours[side : side + 1].astype(F32)
+        own = _iota((TILE, TILE), 0) == _iota((TILE, TILE), 1)
+        tile = jnp.sum(jnp.where(own, line, 0.0), axis=1, keepdims=True).astype(jnp.int32)
         rows = _dot(_onehot(lane == (tile >> 4)), edges)
         at = base + (tile & 15)
         found.append(
@@ -215,34 +217,58 @@
     return [_dot(put[j], turned).astype(BF16) for j in range(2)]
 
 
-def pair_rows(foot):
-    row = _iota((L, L), 0)
-    left = jnp.where(row < L // 2, foot, 0.0).astype(BF16)
-    right = jnp.where(row >= L // 2, foot, 0.0).astype(BF16)
-    return jnp.concatenate([left, right], axis=1)
-
-
-RHS_STEP = 16
+CHUNK = 16
 NORMAL_STEP = 8
-APPLY_STEP = 16
-
-
-def rhs_kernel(tile_ref, offset_ref, tod_ref, weight_ref, beam_ref, message_ref, back, scratch):
-    g = pl.program_id(0)
-    weighted = (weight_ref[...] * tod_ref[...].astype(F32)).astype(BF16)
-    row = _iota((RHS_STEP, FOOT), 0)
-    out = jnp.zeros((RHS_STEP, FOOT), F32)
-    for k in range(RHS_STEP):
-        out = jnp.where(row == k, _dot(weighted, beam_ref[k]), out)
-    back[pl.ds(pl.multiple_of(g * RHS_STEP, RHS_STEP), RHS_STEP), :] = out
-
-    @pl.when(g == pl.num_programs(0) - 1)
-    def _():
-        tile_row = _as_row(tile_ref[...], scratch)
-        offset_row = _as_row(offset_ref[...], scratch)
-        parts = first_message(tile_row, offset_row, back[...])
-        for k in range(3):
-            message_ref[k] = parts[k]
+GROUP = 8
+
+
+def rhs_kernel(
+    tile_hbm, offset_hbm, tod_hbm, weight_hbm, beam_hbm, message_ref,
+    tile_ref, offset_ref, tod_ref, weight_ref, beam_ref, weighted, back, scratch, small_sems, sems,
+):
+    small = [
+        pltpu.make_async_copy(src, dst, small_sems.at[k])
+        for k, (src, dst) in enumerate(
+            (
+                (tod_hbm, tod_ref),
+                (weight_hbm, weight_ref),
+                (tile_hbm, tile_ref),
+                (offset_hbm, offset_ref),
+            )
+        )
+    ]
+    chunks = L // CHUNK
+
+    def beam_copy(c):
+        at = pl.ds(pl.multiple_of(c * CHUNK, CHUNK), CHUNK)
+        return pltpu.make_async_copy(beam_hbm.at[at], beam_ref.at[at], sems.at[c])
+
+    for copy in small:
+        copy.start()
+    for c in range(chunks):
+        beam_copy(c).start()
+    for copy in small:
+        copy.wait()
+    weighted[...] = (weight_ref[...] * tod_ref[...].astype(F32)).astype(BF16)
+    row = _iota((CHUNK, FOOT), 0)
+
+    @pl.loop(0, chunks)
+    def _(c):
+        beam_copy(c).wait()
+        first = pl.multiple_of(c * CHUNK, CHUNK)
+        left = weighted[pl.ds(first, CHUNK), :]
+        out = jnp.zeros((CHUNK, FOOT), F32)
+        for k in range(0, CHUNK, 2):
+            two = jnp.concatenate([beam_ref[first + k], beam_ref[first + k + 1]], axis=1)
+            found = _dot(left, two)
+            out = jnp.where(row == k, found[:, :FOOT], jnp.where(row == k + 1, found[:, FOOT:], out))
+        back[pl.ds(first, CHUNK), :] = out
+
+    parts = first_message(
+        _as_row(tile_ref[...], scratch), _as_row(offset_ref[...], scratch), back[...]
+    )
+    for k in range(3):
+        message_ref[k] = parts[k]
 
 
 def normal_kernel(tile_ref, offset_ref, weight_ref, beam_ref, normal_ref, get_ref, put_ref, shift_ref, scratch):
@@ -250,7 +276,9 @@
         for det in range(2):
             beam = beam_ref[det, k]
             turned = beam.astype(F32).T * weight_ref[det, k : k + 1, :]
-            normal_ref[k, :, det * FOOT : (det + 1) * FOOT] = _dot(turned.astype(BF16), beam).astype(BF16)
+            normal_ref[k // 2, det * FOOT : (det + 1) * FOOT, k % 2 * FOOT : (k % 2 + 1) * FOOT] = _dot(
+                turned.astype(BF16), beam
+            ).astype(BF16)
 
     @pl.when(pl.program_id(0) == 0)
     def _():
@@ -261,6 +289,36 @@
             get_ref[j] = get[j]
             put_ref[j] = put[j]
         shift_ref[...] = shift
+
+
+def fetch_normal(normal_hbm, normal, sems):
+    quads = GROUP // 2
+
+    def copy(g):
+        at = pl.ds(g * quads, quads)
+        return pltpu.make_async_copy(normal_hbm.at[at], normal.at[at], sems.at[g])
+
+    return [copy(g) for g in range(L // 2 // GROUP)]
+
+
+def apply_normal(copies, normal, foot, back):
+    row = _iota((2 * GROUP, FOOT), 0) & (GROUP - 1)
+    none = jnp.zeros((GROUP, FOOT), F32)
+    half = L // 2
+    for g in range(half // GROUP):
+        first = foot[g * GROUP : (g + 1) * GROUP]
+        second = foot[half + g * GROUP : half + (g + 1) * GROUP]
+        left = jnp.concatenate(
+            [jnp.concatenate([first, none], axis=0), jnp.concatenate([none, second], axis=0)], axis=1
+        ).astype(BF16)
+        out = jnp.zeros((2 * GROUP, FOOT), F32)
+        copies[g].wait()
+        for k in range(0, GROUP, 2):
+            found = _dot(left, normal[(g * GROUP + k) // 2])
+            out = jnp.where(row == k, found[:, :FOOT], jnp.where(row == k + 1, found[:, FOOT:], out))
+        back[g * GROUP : (g + 1) * GROUP] = out[:GROUP]
+        back[half + g * GROUP : half + (g + 1) * GROUP] = out[GROUP:]
+    return back[...]
 
 
 def start_kernel(got_ref, field_ref, message_ref, pick_ref, place_ref, shift_ref):
@@ -278,33 +336,20 @@
         shift_ref[j] = shifts[j]
 
 
-def apply_step(normal_ref, pairs, back):
-    g = pl.program_id(0)
-    lane = _iota((L, L), 1) & 63
-    out = _dot_nt(normal_ref[...].reshape(APPLY_STEP * L, 2 * L), pairs[...])
-    acc = back[...]
-    for k in range(APPLY_STEP):
-        acc = jnp.where(lane == g * APPLY_STEP + k, out[k * L : (k + 1) * L], acc)
-    back[...] = acc
-
-
-def first_apply_kernel(got_ref, get_ref, put_ref, shift_ref, normal_ref, message_ref, foot_ref, pairs, back):
-    g = pl.program_id(0)
-
-    @pl.when(g == 0)
-    def _():
-        foot = take_reply((got_ref[0], got_ref[1]), (get_ref[0], get_ref[1]), shift_ref[...])
-        foot_ref[...] = foot
-        pairs[...] = pair_rows(foot)
-        back[...] = jnp.zeros((L, L), F32)
-
-    apply_step(normal_ref, pairs, back)
-
-    @pl.when(g == pl.num_programs(0) - 1)
-    def _():
-        parts = send_back(back[...].T, (put_ref[0], put_ref[1]), shift_ref[...])
-        message_ref[0] = parts[0]
-        message_ref[1] = parts[1]
+def first_apply_kernel(
+    got_ref, get_ref, put_ref, shift_ref, normal_hbm, message_ref, foot_ref, back, normal, sems
+):
+    copies = fetch_normal(normal_hbm, normal, sems)
+    for copy in copies:
+        copy.start()
+    shift = shift_ref[...]
+    foot = take_reply((got_ref[0], got_ref[1]), (get_ref[0], get_ref[1]), shift)
+    foot_ref[...] = foot
+    parts = send_back(
+        apply_normal(copies, normal, foot, back), (put_ref[0], put_ref[1]), shift
+    )
+    message_ref[0] = parts[0]
+    message_ref[1] = parts[1]
 
 
 def middle_kernel(got_ref, before_ref, field_ref, neighbour_ref, pick_ref, place_ref, shift_ref, image_ref, prior_ref, message_ref):
@@ -329,39 +374,32 @@
 
 
 def second_apply_kernel(
-    got_ref, get_ref, put_ref, shift_ref, normal_ref, foot_ref, field_ref, image_ref, smooth_ref, neighbour_ref,
-    message_ref, residual_ref, prior_ref, sums_ref, pairs, back, foot_scr,
+    got_ref, get_ref, put_ref, shift_ref, normal_hbm, foot_ref, field_ref, image_ref, smooth_ref, neighbour_ref,
+    message_ref, residual_ref, prior_ref, sums_ref, back, normal, sems,
 ):
-    g = pl.program_id(0)
-
-    @pl.when(g == 0)
-    def _():
-        sums = jnp.sum(got_ref[2].astype(F32), axis=0, keepdims=True)
-        sums_ref[...] = sums
-        step = _whole(sums, SCALARS) / _whole(sums, SCALARS + 3)
-        taken = take_reply((got_ref[0], got_ref[1]), (get_ref[0], get_ref[1]), shift_ref[...])
-        foot = (foot_ref[...] - step * taken).astype(BF16).astype(F32)
-        foot_scr[...] = foot
-        pairs[...] = pair_rows(foot)
-        back[...] = jnp.zeros((L, L), F32)
-        image = image_ref[...]
-        before, after = outer_edges(got_ref[2], neighbour_ref[...])
-        residual_ref[...] = field_ref[...] - step * image
-        prior_ref[...] = smooth_ref[...] - step * prior(image, before, after)
-
-    apply_step(normal_ref, pairs, back)
-
-    @pl.when(g == pl.num_programs(0) - 1)
-    def _():
-        turned = back[...].T
-        parts = send_back(turned, (put_ref[0], put_ref[1]), shift_ref[...])
-        message_ref[0] = parts[0]
-        message_ref[1] = parts[1]
-        residual = residual_ref[...]
-        square = _total(residual * residual)
-        product = _total(foot_scr[...] * turned + residual * prior_ref[...])
-        extra = _pieces(square, SCALARS) + _pieces(product, SCALARS + 3)
-        message_ref[2] = jnp.broadcast_to(extra, (L, L)).astype(BF16)
+    copies = fetch_normal(normal_hbm, normal, sems)
+    for copy in copies:
+        copy.start()
+    shift = shift_ref[...]
+    sums = jnp.sum(got_ref[2].astype(F32), axis=0, keepdims=True)
+    sums_ref[...] = sums
+    step = _whole(sums, SCALARS) / _whole(sums, SCALARS + 3)
+    taken = take_reply((got_ref[0], got_ref[1]), (get_ref[0], get_ref[1]), shift)
+    foot = (foot_ref[...] - step * taken).astype(BF16).astype(F32)
+    image = image_ref[...]
+    before, after = outer_edges(got_ref[2], neighbour_ref[...])
+    residual = field_ref[...] - step * image
+    smooth = smooth_ref[...] - step * prior(image, before, after)
+    residual_ref[...] = residual
+    prior_ref[...] = smooth
+    turned = apply_normal(copies, normal, foot, back)
+    parts = send_back(turned, (put_ref[0], put_ref[1]), shift)
+    message_ref[0] = parts[0]
+    message_ref[1] = parts[1]
+    square = _total(residual * residual)
+    product = _total(foot * turned + residual * smooth)
+    extra = _pieces(square, SCALARS) + _pieces(product, SCALARS + 3)
+    message_ref[2] = jnp.broadcast_to(extra, (L, L)).astype(BF16)
 
 
 def last_kernel(got_ref, place_ref, shift_ref, field_ref, image_ref, residual_ref, smooth_ref, sums_ref, solution_ref, rest_ref):
@@ -396,25 +434,36 @@
 WIDE = _shape(MAP, F32)
 
 
-def call(kernel, grid, in_specs, outs, out_specs, scratch, args, flops, size):
+def call(kernel, grid, in_specs, outs, out_specs, scratch, args, flops, size, vmem):
     return pl.pallas_call(
         kernel,
-        grid=(grid,),
+        grid=grid,
         in_specs=in_specs,
         out_specs=out_specs,
         out_shape=outs,
         scratch_shapes=scratch,
-        compiler_params=pltpu.CompilerParams(
-            dimension_semantics=("arbitrary",), vmem_limit_bytes=40 * 2**20
-        ),
+        compiler_params=pltpu.CompilerParams(vmem_limit_bytes=vmem * 2**20),
         cost_estimate=pl.CostEstimate(flops=flops, bytes_accessed=size, transcendentals=0),
     )(*args)
 
 
-def whole_call(kernel, outs, args, scratch=()):
-    return call(
-        kernel, 1, [_full(a.shape) for a in args], outs, [_full(o.shape) for o in outs], scratch, args, 2**25, 2**19
-    )
+def whole_call(kernel, outs, args, scratch=(), flops=2**25, size=2**19, hbm=()):
+    vmem = pl.BlockSpec(memory_space=pltpu.VMEM)
+    specs = [
+        pl.BlockSpec(memory_space=pltpu.HBM) if k in hbm else vmem for k in range(len(args))
+    ]
+    return call(kernel, (), specs, outs, [vmem] * len(outs), scratch, args, flops, size, 8)
+
+
+NORMAL_SCRATCH = [
+    pltpu.VMEM(MAP, F32),
+    pltpu.VMEM((L // 4, 2 * FOOT, 2 * FOOT), BF16),
+    pltpu.SemaphoreType.DMA((L // 2 // GROUP,)),
+]
+
+
+def in_hbm(x):
+    return pltpu.with_memory_space_constraint(x, pltpu.HBM)
 
 
 def exchange(x):
@@ -422,58 +471,68 @@
 
 
 def per_device(tod, pointing, weights, tile_ids, offsets, neighbours):
-    ids = [_full(tile_ids.shape)] * 2
     half = L // 2
+    neighbours = neighbours.T
 
     (message,) = call(
         rhs_kernel,
-        L // RHS_STEP,
-        ids
-        + [
-            pl.BlockSpec((RHS_STEP, SAMP), lambda g: (g, 0)),
-            pl.BlockSpec((RHS_STEP, SAMP), lambda g: (g, 0)),
-            pl.BlockSpec((RHS_STEP, SAMP, FOOT), lambda g: (g, 0, 0)),
+        (),
+        [pl.BlockSpec(memory_space=pltpu.HBM)] * 5,
+        [_shape((3, L, L), BF16)],
+        [pl.BlockSpec(memory_space=pltpu.VMEM)],
+        [
+            pltpu.VMEM(tile_ids.shape, jnp.int32),
+            pltpu.VMEM(offsets.shape, jnp.int32),
+            pltpu.VMEM((L, SAMP), BF16),
+            pltpu.VMEM((L, SAMP), F32),
+            pltpu.VMEM((L, SAMP, FOOT), BF16),
+            pltpu.VMEM((L, SAMP), BF16),
+            pltpu.VMEM((L, FOOT), F32),
+            pltpu.VMEM((8, L), F32),
+            pltpu.SemaphoreType.DMA((4,)),
+            pltpu.SemaphoreType.DMA((L // CHUNK,)),
         ],
-        [_shape((3, L, L), BF16)],
-        [_full((3, L, L))],
-        [pltpu.VMEM((L, FOOT), F32), pltpu.VMEM((8, L), F32)],
         (
-            tile_ids,
-            offsets,
-            tod.reshape(L, SAMP),
-            weights.reshape(L, SAMP),
-            pointing.reshape(L, SAMP, FOOT),
+            in_hbm(tile_ids),
+            in_hbm(offsets),
+            in_hbm(tod.reshape(L, SAMP)),
+            in_hbm(weights.reshape(L, SAMP)),
+            in_hbm(pointing.reshape(L, SAMP, FOOT)),
         ),
         2**24,
         2**23,
+        16,
     )
     got = exchange(message)
 
     normal, get, put, shift = call(
         normal_kernel,
-        half // NORMAL_STEP,
-        ids
+        (half // NORMAL_STEP,),
+        [_full(tile_ids.shape)] * 2
         + [
             pl.BlockSpec((2, NORMAL_STEP, SAMP), lambda g: (0, g, 0)),
             pl.BlockSpec((2, NORMAL_STEP, SAMP, FOOT), lambda g: (0, g, 0, 0)),
         ],
         [
-            _shape((half, FOOT, 2 * FOOT), BF16),
+            pltpu.HBM((half // 2, 2 * FOOT, 2 * FOOT), BF16),
             _shape((2, L, L), BF16),
             _shape((2, L, L), BF16),
             _shape((L, L), jnp.int32),
         ],
         [
-            pl.BlockSpec((NORMAL_STEP, FOOT, 2 * FOOT), lambda g: (g, 0, 0)),
+            pl.BlockSpec((NORMAL_STEP // 2, 2 * FOOT, 2 * FOOT), lambda g: (g, 0, 0)),
             _full((2, L, L)),
             _full((2, L, L)),
             _full((L, L)),
         ],
         [pltpu.VMEM((8, L), F32)],
-        (tile_ids, offsets, weights, pointing),
+        (tile_ids, offsets, weights, in_hbm(pointing)),
         2**30,
         12 * 2**20,
-    )
+        16,
+    )
+    normal = in_hbm(normal)
+    got, get, put, shift = lax.optimization_barrier((got, get, put, shift))
 
     field, message, pick, place, shifts = whole_call(
         start_kernel,
@@ -482,18 +541,14 @@
     )
     got_first = exchange(message)
 
-    normal_spec = pl.BlockSpec((APPLY_STEP, FOOT, 2 * FOOT), lambda g: (g, 0, 0))
-    table_specs = [_full((2, L, L)), _full((2, L, L)), _full((L, L)), normal_spec]
-    message, foot = call(
+    message, foot = whole_call(
         first_apply_kernel,
-        half // APPLY_STEP,
-        [_full((3, L, L))] + table_specs,
         [_shape((2, L, L), BF16), WIDE],
-        [_full((2, L, L)), _full(MAP)],
-        [pltpu.VMEM((L, 2 * L), BF16), pltpu.VMEM(MAP, F32)],
         (got_first, get, put, shift, normal),
-        2**29,
+        NORMAL_SCRATCH,
+        2**28,
         2**22,
+        (4,),
     )
     got = exchange(message)
 
@@ -504,16 +559,14 @@
     )
     got = exchange(message)
 
-    message, residual, smooth, sums = call(
+    message, residual, smooth, sums = whole_call(
         second_apply_kernel,
-        half // APPLY_STEP,
-        [_full((3, L, L))] + table_specs + [_full(MAP)] * 4 + [_full(neighbours.shape)],
         [_shape((3, L, L), BF16), WIDE, WIDE, _shape((1, L), F32)],
-        [_full((3, L, L)), _full(MAP), _full(MAP), _full((1, L))],
-        [pltpu.VMEM((L, 2 * L), BF16), pltpu.VMEM(MAP, F32), pltpu.VMEM(MAP, F32)],
         (got, get, put, shift, normal, foot, field, image, smooth, neighbours),
-        2**29,
+        NORMAL_SCRATCH,
+        2**28,
         2**22,
+        (4,),
     )
     got = exchange(message)
 

time: 109 us -> 100 us (0.917)
  local copies, waits for them, and re-layouts: 18 us -> 1.16 us
  blocking collectives: 50.1 us -> 61.9 us
  waiting for transfers between devices: 9.19 us -> 0.13 us
  Pallas kernels: 16.5 us -> 24.6 us
  starting transfers between devices: 14.3 us -> 11.5 us
    unnamed x27 -> x8, local copies, waits for them, and re-layouts: 16.3 us -> 0.02 us
    all_to_all x3 -> x4, blocking collectives: 50.1 us -> 61.9 us  [exchange(): return lax.all_to_all(x, DET_TM, split_axis=1, concat_axis=1, tiled=True)]
    all_to_all x2 -> x1, waiting for transfers between devices: 9.19 us -> 0.13 us  [exchange(): return lax.all_to_all(x, DET_TM, split_axis=1, concat_axis=1, tiled=True)]
    pallas_call x7, Pallas kernels: 16.5 us -> 24.6 us  [call(): pl.pallas_call(kernel, grid=grid, in_specs=in_specs, out_specs=out_specs,...]
    all_to_all x2 -> x1, starting transfers between devices: 14.3 us -> 11.5 us  [exchange(): return lax.all_to_all(x, DET_TM, split_axis=1, concat_axis=1, tiled=True)]
  transfers between devices with their start and end apart: 2 -> 1, of which waited for: 1 -> 1; matrix products, arithmetic and copies ran while one was open for 0% -> 0% of each run, Pallas kernels for 5% -> 10%
where the time goes in v2:
time: 100 us
  blocking collectives  61.9 us (62%)
  Pallas kernels  24.6 us (25%)
  starting transfers between devices  11.5 us (12%)
  local copies, waits for them, and re-layouts  1.16 us (1%)
    all_to_all x4, blocking collectives, exchange(): return lax.all_to_all(x, DET_TM, split_axis=1, concat_axis=1, tiled=True)  61.9 us
    pallas_call x7, Pallas kernels, call(): pl.pallas_call(kernel, grid=grid, in_specs=in_specs, out_specs=out_specs,...  24.6 us
    all_to_all x1, starting transfers between devices, exchange(): return lax.all_to_all(x, DET_TM, split_axis=1, concat_axis=1, tiled=True)  11.5 us
  transfers between devices with their start and end apart: 1, of which 1 were waited for; matrix products, arithmetic and copies ran while one was open for 0% of the time, Pallas kernels for 10%

profile of v2, /device:TPU:1, one launch (start us, length us, event | category | flops | bytes accessed | tf_op | source)
XLA Modules:
  0.0 100.0 jit_solution(5070786717618991952)
XLA Ops:
  0.6 0.0 copy-start.2
  0.6 0.0 copy-start.1
  0.7 0.0 copy-start
  0.7 6.2 %shard_map.77 = bf16[3,128,128]{2,1,0:T(8,128)(2,1)S(1)} custom-call(s32[2,64]{1,0:T(2,128)} %tile_ref.1, s32[2,64]{1,0:T(2,128)} %offset_ref.1, bf16[128,256]{1,0:T(8,128)(2,1)} %bitcast.8, f32[128,256]{1,0:T(8,128)} %bitcast.4, bf16[128,256,128]{2,1,0:T(8,128)(2,1)} %bitcast.7), custom_call_target="tpu_custom_call" | custom-call | flops 16777216 | bytes 8388608 | tf_op jit(solution)/shard_map/pallas_call | solution.py:438
  6.8 0.0 copy-start.3
  6.9 0.7 copy.8
  7.6 11.5 %all-to-all-start = ((bf16[3,128,128]{2,0,1:T(4,128)(2,1)}), bf16[3,128,128]{2,0,1:T(4,128)(2,1)S(1)}, u32[]{:S(2)}, u32[]{:S(2)}) async-start(bf16[3,128,128]{2,0,1:T(4,128)(2,1)} %copy.8), calls=%async_computation | async-start | bytes 262144 | tf_op jit(solution)/shard_map/all_to_all | solution.py:470
  19.1 0.0 copy-done.2
  19.1 0.0 copy-done.1
  19.1 0.0 copy-done
  19.1 9.6 %shard_map.78 = (bf16[32,256,256]{2,1,0:T(8,128)(2,1)}, bf16[2,128,128]{2,1,0:T(8,128)(2,1)S(1)}, bf16[2,128,128]{2,1,0:T(8,128)(2,1)S(1)}, s32[128,128]{1,0:T(8,128)S(1)}) custom-call(s32[2,64]{1,0:T(2,128)S(1)} %copy-done.1, s32[2,64]{1,0:T(2,128)S(1)} %copy-done.2, f32[2,64,256]{2,1,0:T(8,128)S(1)} %copy-done, bf16[2,64,256,128]{3,2,1,0:T(8,128)(2,1)} %beam_ref.1), custom_call_target="tpu_custom_call" | custom-call | flops 1073741824 | bytes 12582912 | tf_op jit(solution)/shard_map/pallas_call | solution.py:438
  28.7 0.1 all-to-all-done
  28.9 0.5 shard_map.79
  29.3 0.1 copy.10
  29.4 19.4 %all_to_all.25 = bf16[3,128,128]{2,0,1:T(4,128)(2,1)S(1)} all-to-all(bf16[3,128,128]{2,0,1:T(4,128)(2,1)S(1)} %copy.10), channel_id=1, replica_groups=mesh['det'=4,'tm_0'=4,'tm_1'=4,'tm_2'=2] {'det','tm_0','tm_1','tm_2'}, dimensions={1} | all-to-all | bytes 196608 | tf_op jit(solution)/shard_map/all_to_all | solution.py:470
  48.9 3.3 %shard_map.80 = (bf16[2,128,128]{2,1,0:T(8,128)(2,1)S(1)}, f32[128,128]{1,0:T(8,128)S(1)}) custom-call(bf16[3,128,128]{2,1,0:T(8,128)(2,1)S(1)} %copy.11.got_ref.before_ref, bf16[2,128,128]{2,1,0:T(8,128)(2,1)S(1)} %get-tuple-element.29.get_ref, bf16[2,128,128]{2,1,0:T(8,128)(2,1)S(1)} %get-tuple-element.30.put_ref, ...), custom_call_target="tpu_custom_call" | custom-call | flops 268435456 | bytes 4194304 | tf_op jit(solution)/shard_map/pallas_call | solution.py:438
  52.1 0.1 copy.12
  52.2 13.7 %all_to_all.26 = bf16[2,128,128]{2,0,1:T(2,128)(2,1)S(1)} all-to-all(bf16[2,128,128]{2,0,1:T(2,128)(2,1)S(1)} %copy.12), channel_id=1, replica_groups=mesh['det'=4,'tm_0'=4,'tm_1'=4,'tm_2'=2] {'det','tm_0','tm_1','tm_2'}, dimensions={1} | all-to-all | bytes 131072 | tf_op jit(solution)/shard_map/all_to_all | solution.py:470
  65.9 0.0 copy-done.3
  65.9 0.6 shard_map.81
  66.5 0.1 copy.15
  66.6 14.5 %all_to_all.27 = bf16[3,128,128]{2,0,1:T(4,128)(2,1)S(1)} all-to-all(bf16[3,128,128]{2,0,1:T(4,128)(2,1)S(1)} %copy.15), channel_id=1, replica_groups=mesh['det'=4,'tm_0'=4,'tm_1'=4,'tm_2'=2] {'det','tm_0','tm_1','tm_2'}, dimensions={1} | all-to-all | bytes 196608 | tf_op jit(solution)/shard_map/all_to_all | solution.py:470
  81.1 3.7 %shard_map.82 = (bf16[3,128,128]{2,1,0:T(8,128)(2,1)S(1)}, f32[128,128]{1,0:T(8,128)S(1)}, f32[128,128]{1,0:T(8,128)S(1)}, f32[1,128]{1,0:T(1,128)S(1)}) custom-call(bf16[3,128,128]{2,1,0:T(8,128)(2,1)S(1)} %copy.16.got_ref, bf16[2,128,128]{2,1,0:T(8,128)(2,1)S(1)} %get-tuple-element.29.get_ref, bf16[2,128,128]{2,1,0:T(8,128)(2,1)S(1)} %get-tuple-element.30.put_ref, ...), custom_call_target="tpu_custom_call" | custom-call | flops 268435456 | bytes 4194304 | tf_op jit(solution)/shard_map/pallas_call | solution.py:438
  84.8 0.1 copy.17
  84.9 14.3 %all_to_all.28 = bf16[3,128,128]{2,0,1:T(4,128)(2,1)S(1)} all-to-all(bf16[3,128,128]{2,0,1:T(4,128)(2,1)S(1)} %copy.17), channel_id=1, replica_groups=mesh['det'=4,'tm_0'=4,'tm_1'=4,'tm_2'=2] {'det','tm_0','tm_1','tm_2'}, dimensions={1} | all-to-all | bytes 196608 | tf_op jit(solution)/shard_map/all_to_all | solution.py:470
  99.2 0.8 shard_map.83
  (5 shorter events, 0.1 us)
Async XLA Ops:
  0.6 18.5 %copy-start.2 = (s32[2,64]{1,0:T(2,128)S(1)}, s32[2,64]{1,0:T(2,128)}, u32[]{:S(2)}) copy-start(s32[2,64]{1,0:T(2,128)} %offset_ref.1) | copy-start | bytes 1540
  0.6 18.5 %copy-start.1 = (s32[2,64]{1,0:T(2,128)S(1)}, s32[2,64]{1,0:T(2,128)}, u32[]{:S(2)}) copy-start(s32[2,64]{1,0:T(2,128)} %tile_ref.1) | copy-start | bytes 1540
  0.7 18.5 %copy-start = (f32[2,64,256]{2,1,0:T(8,128)S(1)}, f32[2,64,256]{2,1,0:T(8,128)}, u32[]{:S(2)}) copy-start(f32[2,64,256]{2,1,0:T(8,128)} %weight_ref.1) | copy-start | bytes 393220
  6.8 59.0 %copy-start.3 = (s32[16,2]{0,1:T(2,128)S(1)}, s32[16,2]{0,1:T(2,128)}, u32[]{:S(2)}) copy-start(s32[16,2]{0,1:T(2,128)} %param.11) | copy-start | bytes 388
  7.6 21.3 %all-to-all-start = ((bf16[3,128,128]{2,0,1:T(4,128)(2,1)}), bf16[3,128,128]{2,0,1:T(4,128)(2,1)S(1)}, u32[]{:S(2)}, u32[]{:S(2)}) async-start(bf16[3,128,128]{2,0,1:T(4,128)(2,1)} %copy.8), calls=%async_computation | async-start | bytes 262144 | tf_op jit(solution)/shard_map/all_to_all | solution.py:470

commit v3 on v2

--- a/solution.py
+++ b/solution.py
@@ -92,28 +92,18 @@
     return _onehot((_iota((L, L), 0) == owner_row) & ((block & 1) == j))
 
 
-def first_message(tile_row, offset_row, back):
+def places(tile_row, offset_row, put):
     tile = tile_row.astype(jnp.int32)
     offset = offset_row.astype(jnp.int32)
-    owner = tile >> 4
     start_row = (offset >> 7) * ROW_STEP + (tile & 15)
-    shift = offset & 127
-    shift_col = _to_col(shift.astype(F32)).astype(jnp.int32)
-    turned = _rotate(back, shift_col).astype(BF16)
-    to_0 = _blocks_of(owner, 0)
-    to_1 = _blocks_of(owner, 1)
     line = _iota((L, L), 0)
     place = 2 * (_iota((L, L), 1) & 1)
     facts = jnp.where(
         line == place,
         start_row.astype(F32),
-        jnp.where(line == place + 1, shift.astype(F32), 0.0),
+        jnp.where(line == place + 1, (offset & 127).astype(F32), 0.0),
     ).astype(BF16)
-    return (
-        _dot(to_0, turned).astype(BF16),
-        _dot(to_1, turned).astype(BF16),
-        _dot_nt(to_0 + to_1, facts).astype(BF16),
-    )
+    return _dot_nt(put[0] + put[1], facts).astype(BF16)
 
 
 def block_tables(tile_row, offset_row):
@@ -218,106 +208,91 @@
 
 
 CHUNK = 16
-NORMAL_STEP = 8
-GROUP = 8
+STEPS = (32, 32, 32, 32)
+DEPTH = 2
 
 
 def rhs_kernel(
-    tile_hbm, offset_hbm, tod_hbm, weight_hbm, beam_hbm, message_ref,
+    tile_hbm, offset_hbm, tod_hbm, weight_hbm, beam_hbm,
+    message_ref, normal_ref, get_ref, put_ref, shift_ref,
     tile_ref, offset_ref, tod_ref, weight_ref, beam_ref, weighted, back, scratch, small_sems, sems,
 ):
     small = [
         pltpu.make_async_copy(src, dst, small_sems.at[k])
         for k, (src, dst) in enumerate(
             (
+                (tile_hbm, tile_ref),
+                (offset_hbm, offset_ref),
                 (tod_hbm, tod_ref),
                 (weight_hbm, weight_ref),
-                (tile_hbm, tile_ref),
-                (offset_hbm, offset_ref),
             )
         )
     ]
-    chunks = L // CHUNK
-
-    def beam_copy(c):
-        at = pl.ds(pl.multiple_of(c * CHUNK, CHUNK), CHUNK)
-        return pltpu.make_async_copy(beam_hbm.at[at], beam_ref.at[at], sems.at[c])
+    starts = [sum(STEPS[:k]) for k in range(len(STEPS))]
+    beams = [
+        pltpu.make_async_copy(
+            beam_hbm.at[pl.ds(first, size)], beam_ref.at[pl.ds(first, size)], sems.at[k]
+        )
+        for k, (first, size) in enumerate(zip(starts, STEPS))
+    ]
 
     for copy in small:
         copy.start()
-    for c in range(chunks):
-        beam_copy(c).start()
-    for copy in small:
-        copy.wait()
+    for copy in beams[:DEPTH]:
+        copy.start()
+    small[0].wait()
+    small[1].wait()
+    tile_row = _as_row(tile_ref[...], scratch)
+    offset_row = _as_row(offset_ref[...], scratch)
+    get, put, shift = block_tables(tile_row, offset_row)
+    for j in range(2):
+        get_ref[j] = get[j]
+        put_ref[j] = put[j]
+    shift_ref[...] = shift
+    message_ref[2] = places(tile_row, offset_row, put)
+    small[2].wait()
+    small[3].wait()
     weighted[...] = (weight_ref[...] * tod_ref[...].astype(F32)).astype(BF16)
     row = _iota((CHUNK, FOOT), 0)
 
-    @pl.loop(0, chunks)
-    def _(c):
-        beam_copy(c).wait()
-        first = pl.multiple_of(c * CHUNK, CHUNK)
-        left = weighted[pl.ds(first, CHUNK), :]
+    for step, (start, size) in enumerate(zip(starts, STEPS)):
+        beams[step].wait()
+        if step + DEPTH < len(STEPS):
+            beams[step + DEPTH].start()
+        for first in range(start, start + size, CHUNK):
+            rows = weighted[first : first + CHUNK]
+            weight = weight_ref[first : first + CHUNK]
+            out = jnp.zeros((CHUNK, FOOT), F32)
+            for k in range(CHUNK):
+                beam = beam_ref[first + k]
+                turned = (beam.T.astype(F32) * weight[k : k + 1]).astype(BF16)
+                found = _dot(jnp.concatenate([turned, rows], axis=0), beam)
+                down, across = k % 2 * FOOT, k // 2 % 2 * FOOT
+                normal_ref[(first + k) // 4, down : down + FOOT, across : across + FOOT] = found[
+                    :FOOT
+                ].astype(BF16)
+                out = jnp.where(row == k, found[FOOT:], out)
+            back[first : first + CHUNK] = out
+
+    parts = send_back(back[...], put, shift)
+    message_ref[0] = parts[0]
+    message_ref[1] = parts[1]
+
+
+def apply_normal(normal_ref, foot, back):
+    row = _iota((CHUNK, FOOT), 0)
+    for c in range(L // CHUNK):
+        own = foot[c * CHUNK : (c + 1) * CHUNK]
+        left = jnp.concatenate(
+            [jnp.where((row & 1) == 0, own, 0.0), jnp.where((row & 1) == 1, own, 0.0)], axis=1
+        ).astype(BF16)
         out = jnp.zeros((CHUNK, FOOT), F32)
-        for k in range(0, CHUNK, 2):
-            two = jnp.concatenate([beam_ref[first + k], beam_ref[first + k + 1]], axis=1)
-            found = _dot(left, two)
-            out = jnp.where(row == k, found[:, :FOOT], jnp.where(row == k + 1, found[:, FOOT:], out))
-        back[pl.ds(first, CHUNK), :] = out
-
-    parts = first_message(
-        _as_row(tile_ref[...], scratch), _as_row(offset_ref[...], scratch), back[...]
-    )
-    for k in range(3):
-        message_ref[k] = parts[k]
-
-
-def normal_kernel(tile_ref, offset_ref, weight_ref, beam_ref, normal_ref, get_ref, put_ref, shift_ref, scratch):
-    for k in range(NORMAL_STEP):
-        for det in range(2):
-            beam = beam_ref[det, k]
-            turned = beam.astype(F32).T * weight_ref[det, k : k + 1, :]
-            normal_ref[k // 2, det * FOOT : (det + 1) * FOOT, k % 2 * FOOT : (k % 2 + 1) * FOOT] = _dot(
-                turned.astype(BF16), beam
-            ).astype(BF16)
-
-    @pl.when(pl.program_id(0) == 0)
-    def _():
-        tile_row = _as_row(tile_ref[...], scratch)
-        offset_row = _as_row(offset_ref[...], scratch)
-        get, put, shift = block_tables(tile_row, offset_row)
-        for j in range(2):
-            get_ref[j] = get[j]
-            put_ref[j] = put[j]
-        shift_ref[...] = shift
-
-
-def fetch_normal(normal_hbm, normal, sems):
-    quads = GROUP // 2
-
-    def copy(g):
-        at = pl.ds(g * quads, quads)
-        return pltpu.make_async_copy(normal_hbm.at[at], normal.at[at], sems.at[g])
-
-    return [copy(g) for g in range(L // 2 // GROUP)]
-
-
-def apply_normal(copies, normal, foot, back):
-    row = _iota((2 * GROUP, FOOT), 0) & (GROUP - 1)
-    none = jnp.zeros((GROUP, FOOT), F32)
-    half = L // 2
-    for g in range(half // GROUP):
-        first = foot[g * GROUP : (g + 1) * GROUP]
-        second = foot[half + g * GROUP : half + (g + 1) * GROUP]
-        left = jnp.concatenate(
-            [jnp.concatenate([first, none], axis=0), jnp.concatenate([none, second], axis=0)], axis=1
-        ).astype(BF16)
-        out = jnp.zeros((2 * GROUP, FOOT), F32)
-        copies[g].wait()
-        for k in range(0, GROUP, 2):
-            found = _dot(left, normal[(g * GROUP + k) // 2])
-            out = jnp.where(row == k, found[:, :FOOT], jnp.where(row == k + 1, found[:, FOOT:], out))
-        back[g * GROUP : (g + 1) * GROUP] = out[:GROUP]
-        back[half + g * GROUP : half + (g + 1) * GROUP] = out[GROUP:]
+        for q in range(CHUNK // 4):
+            found = _dot(left, normal_ref[c * (CHUNK // 4) + q])
+            out = jnp.where(
+                (row >> 1) == 2 * q, found[:, :FOOT], jnp.where((row >> 1) == 2 * q + 1, found[:, FOOT:], out)
+            )
+        back[c * CHUNK : (c + 1) * CHUNK] = out
     return back[...]
 
 
@@ -337,16 +312,13 @@
 
 
 def first_apply_kernel(
-    got_ref, get_ref, put_ref, shift_ref, normal_hbm, message_ref, foot_ref, back, normal, sems
+    got_ref, get_ref, put_ref, shift_ref, normal_ref, message_ref, foot_ref, back
 ):
-    copies = fetch_normal(normal_hbm, normal, sems)
-    for copy in copies:
-        copy.start()
     shift = shift_ref[...]
     foot = take_reply((got_ref[0], got_ref[1]), (get_ref[0], get_ref[1]), shift)
     foot_ref[...] = foot
     parts = send_back(
-        apply_normal(copies, normal, foot, back), (put_ref[0], put_ref[1]), shift
+        apply_normal(normal_ref, foot, back), (put_ref[0], put_ref[1]), shift
     )
     message_ref[0] = parts[0]
     message_ref[1] = parts[1]
@@ -374,12 +346,9 @@
 
 
 def second_apply_kernel(
-    got_ref, get_ref, put_ref, shift_ref, normal_hbm, foot_ref, field_ref, image_ref, smooth_ref, neighbour_ref,
-    message_ref, residual_ref, prior_ref, sums_ref, back, normal, sems,
+    got_ref, get_ref, put_ref, shift_ref, normal_ref, foot_ref, field_ref, image_ref, smooth_ref, neighbour_ref,
+    message_ref, residual_ref, prior_ref, sums_ref, back,
 ):
-    copies = fetch_normal(normal_hbm, normal, sems)
-    for copy in copies:
-        copy.start()
     shift = shift_ref[...]
     sums = jnp.sum(got_ref[2].astype(F32), axis=0, keepdims=True)
     sums_ref[...] = sums
@@ -392,7 +361,7 @@
     smooth = smooth_ref[...] - step * prior(image, before, after)
     residual_ref[...] = residual
     prior_ref[...] = smooth
-    turned = apply_normal(copies, normal, foot, back)
+    turned = apply_normal(normal_ref, foot, back)
     parts = send_back(turned, (put_ref[0], put_ref[1]), shift)
     message_ref[0] = parts[0]
     message_ref[1] = parts[1]
@@ -447,19 +416,11 @@
     )(*args)
 
 
-def whole_call(kernel, outs, args, scratch=(), flops=2**25, size=2**19, hbm=()):
+def whole_call(kernel, outs, args, scratch=(), flops=2**25, size=2**19):
     vmem = pl.BlockSpec(memory_space=pltpu.VMEM)
-    specs = [
-        pl.BlockSpec(memory_space=pltpu.HBM) if k in hbm else vmem for k in range(len(args))
-    ]
-    return call(kernel, (), specs, outs, [vmem] * len(outs), scratch, args, flops, size, 8)
-
-
-NORMAL_SCRATCH = [
-    pltpu.VMEM(MAP, F32),
-    pltpu.VMEM((L // 4, 2 * FOOT, 2 * FOOT), BF16),
-    pltpu.SemaphoreType.DMA((L // 2 // GROUP,)),
-]
+    return call(
+        kernel, (), [vmem] * len(args), outs, [vmem] * len(outs), scratch, args, flops, size, 8
+    )
 
 
 def in_hbm(x):
@@ -471,15 +432,20 @@
 
 
 def per_device(tod, pointing, weights, tile_ids, offsets, neighbours):
-    half = L // 2
     neighbours = neighbours.T
 
-    (message,) = call(
+    message, normal, get, put, shift = call(
         rhs_kernel,
         (),
         [pl.BlockSpec(memory_space=pltpu.HBM)] * 5,
-        [_shape((3, L, L), BF16)],
-        [pl.BlockSpec(memory_space=pltpu.VMEM)],
+        [
+            _shape((3, L, L), BF16),
+            pltpu.VMEM((L // 4, 2 * FOOT, 2 * FOOT), BF16),
+            _shape((2, L, L), BF16),
+            _shape((2, L, L), BF16),
+            _shape((L, L), jnp.int32),
+        ],
+        [pl.BlockSpec(memory_space=pltpu.VMEM)] * 5,
         [
             pltpu.VMEM(tile_ids.shape, jnp.int32),
             pltpu.VMEM(offsets.shape, jnp.int32),
@@ -490,7 +456,7 @@
             pltpu.VMEM((L, FOOT), F32),
             pltpu.VMEM((8, L), F32),
             pltpu.SemaphoreType.DMA((4,)),
-            pltpu.SemaphoreType.DMA((L // CHUNK,)),
+            pltpu.SemaphoreType.DMA((len(STEPS),)),
         ],
         (
             in_hbm(tile_ids),
@@ -499,40 +465,11 @@
             in_hbm(weights.reshape(L, SAMP)),
             in_hbm(pointing.reshape(L, SAMP, FOOT)),
         ),
-        2**24,
+        2**30,
         2**23,
         16,
     )
     got = exchange(message)
-
-    normal, get, put, shift = call(
-        normal_kernel,
-        (half // NORMAL_STEP,),
-        [_full(tile_ids.shape)] * 2
-        + [
-            pl.BlockSpec((2, NORMAL_STEP, SAMP), lambda g: (0, g, 0)),
-            pl.BlockSpec((2, NORMAL_STEP, SAMP, FOOT), lambda g: (0, g, 0, 0)),
-        ],
-        [
-            pltpu.HBM((half // 2, 2 * FOOT, 2 * FOOT), BF16),
-            _shape((2, L, L), BF16),
-            _shape((2, L, L), BF16),
-            _shape((L, L), jnp.int32),
-        ],
-        [
-            pl.BlockSpec((NORMAL_STEP // 2, 2 * FOOT, 2 * FOOT), lambda g: (g, 0, 0)),
-            _full((2, L, L)),
-            _full((2, L, L)),
-            _full((L, L)),
-        ],
-        [pltpu.VMEM((8, L), F32)],
-        (tile_ids, offsets, weights, in_hbm(pointing)),
-        2**30,
-        12 * 2**20,
-        16,
-    )
-    normal = in_hbm(normal)
-    got, get, put, shift = lax.optimization_barrier((got, get, put, shift))
 
     field, message, pick, place, shifts = whole_call(
         start_kernel,
@@ -545,10 +482,9 @@
         first_apply_kernel,
         [_shape((2, L, L), BF16), WIDE],
         (got_first, get, put, shift, normal),
-        NORMAL_SCRATCH,
+        [pltpu.VMEM(MAP, F32)],
         2**28,
         2**22,
-        (4,),
     )
     got = exchange(message)
 
@@ -563,10 +499,9 @@
         second_apply_kernel,
         [_shape((3, L, L), BF16), WIDE, WIDE, _shape((1, L), F32)],
         (got, get, put, shift, normal, foot, field, image, smooth, neighbours),
-        NORMAL_SCRATCH,
+        [pltpu.VMEM(MAP, F32)],
         2**28,
         2**22,
-        (4,),
     )
     got = exchange(message)
 

time: 100 us -> 91.6 us (0.916)
  blocking collectives: 61.9 us -> 78 us
  Pallas kernels: 24.6 us -> 12.2 us
  starting transfers between devices: 11.5 us -> 0 us
    all_to_all x4 -> x5, blocking collectives: 61.9 us -> 78 us  [exchange(): return lax.all_to_all(x, DET_TM, split_axis=1, concat_axis=1, tiled=True)]
    pallas_call x7 -> x6, Pallas kernels: 24.6 us -> 12.2 us  [call(): pl.pallas_call(kernel, grid=grid, in_specs=in_specs, out_specs=out_specs,...]
    all_to_all x1 -> x0, starting transfers between devices: 11.5 us -> none  [exchange(): return lax.all_to_all(x, DET_TM, split_axis=1, concat_axis=1, tiled=True)]
  transfers between devices with their start and end apart: 1 -> 0, of which waited for: 1 -> 0; matrix products, arithmetic and copies ran while one was open for 0% -> 0% of each run, Pallas kernels for 10% -> 0%
where the time goes in v3:
time: 91.6 us; the launch traced here: 91.4 us
  blocking collectives  78 us (85%)
  Pallas kernels  12.2 us (13%)
    all_to_all x5, blocking collectives, exchange(): return lax.all_to_all(x, DET_TM, split_axis=1, concat_axis=1, tiled=True)  78 us
    pallas_call x6, Pallas kernels, call(): pl.pallas_call(kernel, grid=grid, in_specs=in_specs, out_specs=out_specs,...  12.2 us

profile of v3, /device:TPU:1, one launch (start us, length us, event | category | flops | bytes accessed | tf_op | source)
XLA Modules:
  0.0 91.4 jit_solution(11125204668485264073)
XLA Ops:
  0.6 0.0 copy-start
  0.6 5.8 %shard_map.77 = (bf16[3,128,128]{2,1,0:T(8,128)(2,1)S(1)}, bf16[32,256,256]{2,1,0:T(8,128)(2,1)S(1)}, bf16[2,128,128]{2,1,0:T(8,128)(2,1)S(1)}, bf16[2,128,128]{2,1,0:T(8,128)(2,1)S(1)}, s32[128,128]{1,0:T(8,128)S(1)}) custom-call(s32[2,64]{1,0:T(2,128)} %tile_hbm.1, s32[2,64]{1,0:T(2,128)} %offset_hbm.1, bf16[128,256]{1,0:T(8,128)(2,1)} %bitcast.8, ...), custom_call_target="tpu_custom_call" | custom-call | flops 1073741824 | bytes 8388608 | tf_op jit(solution)/shard_map/pallas_call | solution.py:407
  6.4 0.1 copy.8
  6.5 21.3 %all_to_all.25 = bf16[3,128,128]{2,0,1:T(4,128)(2,1)S(1)} all-to-all(bf16[3,128,128]{2,0,1:T(4,128)(2,1)S(1)} %copy.8), channel_id=1, replica_groups=mesh['det'=4,'tm_0'=4,'tm_1'=4,'tm_2'=2] {'det','tm_0','tm_1','tm_2'}, dimensions={1} | all-to-all | bytes 196608 | tf_op jit(solution)/shard_map/all_to_all | solution.py:431
  27.8 0.5 shard_map.78
  28.3 0.1 copy.10
  28.4 14.3 %all_to_all.26 = bf16[3,128,128]{2,0,1:T(4,128)(2,1)S(1)} all-to-all(bf16[3,128,128]{2,0,1:T(4,128)(2,1)S(1)} %copy.10), channel_id=1, replica_groups=mesh['det'=4,'tm_0'=4,'tm_1'=4,'tm_2'=2] {'det','tm_0','tm_1','tm_2'}, dimensions={1} | all-to-all | bytes 196608 | tf_op jit(solution)/shard_map/all_to_all | solution.py:431
  42.7 2.2 %shard_map.79 = (bf16[2,128,128]{2,1,0:T(8,128)(2,1)S(1)}, f32[128,128]{1,0:T(8,128)S(1)}) custom-call(bf16[3,128,128]{2,1,0:T(8,128)(2,1)S(1)} %copy.11.got_ref.before_ref, bf16[2,128,128]{2,1,0:T(8,128)(2,1)S(1)} %get-tuple-element.23.get_ref, bf16[2,128,128]{2,1,0:T(8,128)(2,1)S(1)} %get-tuple-element.24.put_ref, ...), custom_call_target="tpu_custom_call" | custom-call | flops 268435456 | bytes 4194304 | tf_op jit(solution)/shard_map/pallas_call | solution.py:407
  44.9 0.1 copy.12
  45.0 13.7 %all_to_all.27 = bf16[2,128,128]{2,0,1:T(2,128)(2,1)S(1)} all-to-all(bf16[2,128,128]{2,0,1:T(2,128)(2,1)S(1)} %copy.12), channel_id=1, replica_groups=mesh['det'=4,'tm_0'=4,'tm_1'=4,'tm_2'=2] {'det','tm_0','tm_1','tm_2'}, dimensions={1} | all-to-all | bytes 131072 | tf_op jit(solution)/shard_map/all_to_all | solution.py:431
  58.6 0.0 copy-done
  58.6 0.6 shard_map.80
  59.2 0.1 copy.15
  59.3 14.5 %all_to_all.28 = bf16[3,128,128]{2,0,1:T(4,128)(2,1)S(1)} all-to-all(bf16[3,128,128]{2,0,1:T(4,128)(2,1)S(1)} %copy.15), channel_id=1, replica_groups=mesh['det'=4,'tm_0'=4,'tm_1'=4,'tm_2'=2] {'det','tm_0','tm_1','tm_2'}, dimensions={1} | all-to-all | bytes 196608 | tf_op jit(solution)/shard_map/all_to_all | solution.py:431
  73.9 2.3 %shard_map.81 = (bf16[3,128,128]{2,1,0:T(8,128)(2,1)S(1)}, f32[128,128]{1,0:T(8,128)S(1)}, f32[128,128]{1,0:T(8,128)S(1)}, f32[1,128]{1,0:T(1,128)S(1)}) custom-call(bf16[3,128,128]{2,1,0:T(8,128)(2,1)S(1)} %copy.16.got_ref, bf16[2,128,128]{2,1,0:T(8,128)(2,1)S(1)} %get-tuple-element.23.get_ref, bf16[2,128,128]{2,1,0:T(8,128)(2,1)S(1)} %get-tuple-element.24.put_ref, ...), custom_call_target="tpu_custom_call" | custom-call | flops 268435456 | bytes 4194304 | tf_op jit(solution)/shard_map/pallas_call | solution.py:407
  76.2 0.1 copy.17
  76.3 14.3 %all_to_all.29 = bf16[3,128,128]{2,0,1:T(4,128)(2,1)S(1)} all-to-all(bf16[3,128,128]{2,0,1:T(4,128)(2,1)S(1)} %copy.17), channel_id=1, replica_groups=mesh['det'=4,'tm_0'=4,'tm_1'=4,'tm_2'=2] {'det','tm_0','tm_1','tm_2'}, dimensions={1} | all-to-all | bytes 196608 | tf_op jit(solution)/shard_map/all_to_all | solution.py:431
  90.5 0.8 shard_map.82
  (5 shorter events, 0.1 us)
Async XLA Ops:
  0.6 58.0 %copy-start = (s32[16,2]{0,1:T(2,128)S(1)}, s32[16,2]{0,1:T(2,128)}, u32[]{:S(2)}) copy-start(s32[16,2]{0,1:T(2,128)} %param.11) | copy-start | bytes 388

commit v4 on v3

--- a/solution.py
+++ b/solution.py
@@ -9,6 +9,7 @@
 
 DET_TM = ("det", "tm_0", "tm_1", "tm_2")
 TM = ("tm_0", "tm_1", "tm_2")
+SEND = ("tm_2", "tm_1", "tm_0", "det")
 SAMP = 256
 FOOT = 128
 L = 128
@@ -54,8 +55,14 @@
 
 
 def _rotate(x, amount):
-    for bit in range(7):
-        x = jnp.where((amount & (1 << bit)) != 0, _roll(x, 1 << bit, 1), x)
+    step = 1
+    for base in (8, 4, 4):
+        digit = (amount >> (step.bit_length() - 1)) & (base - 1)
+        turned = x
+        for value in range(1, base):
+            turned = jnp.where(digit == value, _roll(x, step * value, 1), turned)
+        x = turned
+        step *= base
     return x
 
 
@@ -85,6 +92,11 @@
 
 def _total(x):
     return jnp.sum(jnp.sum(x, axis=0, keepdims=True), axis=1, keepdims=True)
+
+
+def _owner(tile):
+    det, tm_0, tm_1, tm_2 = tile >> 9, (tile >> 7) & 3, (tile >> 5) & 3, (tile >> 4) & 1
+    return (tm_2 << 6) | (tm_1 << 4) | (tm_0 << 2) | det
 
 
 def _blocks_of(owner_row, j):
@@ -107,7 +119,7 @@
 
 
 def block_tables(tile_row, offset_row):
-    owner = tile_row.astype(jnp.int32) >> 4
+    owner = _owner(tile_row.astype(jnp.int32))
     shift = offset_row.astype(jnp.int32) & 127
     owner_col = _to_col(owner.astype(F32)).astype(jnp.int32)
     shift_col = _to_col(shift.astype(F32)).astype(jnp.int32)
@@ -174,7 +186,7 @@
         line = neighbours[side : side + 1].astype(F32)
         own = _iota((TILE, TILE), 0) == _iota((TILE, TILE), 1)
         tile = jnp.sum(jnp.where(own, line, 0.0), axis=1, keepdims=True).astype(jnp.int32)
-        rows = _dot(_onehot(lane == (tile >> 4)), edges)
+        rows = _dot(_onehot(lane == _owner(tile)), edges)
         at = base + (tile & 15)
         found.append(
             jnp.sum(jnp.where((lane == at) | (lane == at + 16), rows, 0.0), axis=1, keepdims=True)
@@ -428,7 +440,7 @@
 
 
 def exchange(x):
-    return lax.all_to_all(x, DET_TM, split_axis=1, concat_axis=1, tiled=True)
+    return lax.all_to_all(x, SEND, split_axis=1, concat_axis=1, tiled=True)
 
 
 def per_device(tod, pointing, weights, tile_ids, offsets, neighbours):

time: 91.6 us -> 87.7 us (0.957)
  blocking collectives: 78 us -> 75.7 us
  Pallas kernels: 12.2 us -> 10.5 us
    all_to_all x5, blocking collectives: 78 us -> 75.7 us  [exchange(): return lax.all_to_all(x, SEND, split_axis=1, concat_axis=1, tiled=True)]
    pallas_call x6, Pallas kernels: 12.2 us -> 10.5 us  [call(): pl.pallas_call(kernel, grid=grid, in_specs=in_specs, out_specs=out_specs,...]
where the time goes in v4:
time: 87.7 us; the launch traced here: 87.4 us
  blocking collectives  75.7 us (86%)
  Pallas kernels  10.5 us (12%)
    all_to_all x5, blocking collectives, exchange(): return lax.all_to_all(x, SEND, split_axis=1, concat_axis=1, tiled=True)  75.7 us
    pallas_call x6, Pallas kernels, call(): pl.pallas_call(kernel, grid=grid, in_specs=in_specs, out_specs=out_specs,...  10.5 us

profile of v4, /device:TPU:1, one launch (start us, length us, event | category | flops | bytes accessed | tf_op | source)
XLA Modules:
  0.0 87.4 jit_solution(1898166284174932323)
XLA Ops:
  0.6 0.0 copy-start
  0.6 5.5 %shard_map.77 = (bf16[3,128,128]{2,1,0:T(8,128)(2,1)S(1)}, bf16[32,256,256]{2,1,0:T(8,128)(2,1)S(1)}, bf16[2,128,128]{2,1,0:T(8,128)(2,1)S(1)}, bf16[2,128,128]{2,1,0:T(8,128)(2,1)S(1)}, s32[128,128]{1,0:T(8,128)S(1)}) custom-call(s32[2,64]{1,0:T(2,128)} %tile_hbm.1, s32[2,64]{1,0:T(2,128)} %offset_hbm.1, bf16[128,256]{1,0:T(8,128)(2,1)} %bitcast.8, ...), custom_call_target="tpu_custom_call" | custom-call | flops 1073741824 | bytes 8388608 | tf_op jit(solution)/shard_map/pallas_call | solution.py:419
  6.2 0.1 copy.8
  6.3 21.3 %all_to_all.25 = bf16[3,128,128]{2,0,1:T(4,128)(2,1)S(1)} all-to-all(bf16[3,128,128]{2,0,1:T(4,128)(2,1)S(1)} %copy.8), channel_id=1, replica_groups=mesh['det'=4,'tm_0'=4,'tm_1'=4,'tm_2'=2] {'tm_2','tm_1','tm_0','det'}, dimensions={1} | all-to-all | bytes 196608 | tf_op jit(solution)/shard_map/all_to_all | solution.py:443
  27.6 0.5 shard_map.78
  28.1 0.1 copy.10
  28.2 13.7 %all_to_all.26 = bf16[3,128,128]{2,0,1:T(4,128)(2,1)S(1)} all-to-all(bf16[3,128,128]{2,0,1:T(4,128)(2,1)S(1)} %copy.10), channel_id=1, replica_groups=mesh['det'=4,'tm_0'=4,'tm_1'=4,'tm_2'=2] {'tm_2','tm_1','tm_0','det'}, dimensions={1} | all-to-all | bytes 196608 | tf_op jit(solution)/shard_map/all_to_all | solution.py:443
  41.9 1.5 %shard_map.79 = (bf16[2,128,128]{2,1,0:T(8,128)(2,1)S(1)}, f32[128,128]{1,0:T(8,128)S(1)}) custom-call(bf16[3,128,128]{2,1,0:T(8,128)(2,1)S(1)} %copy.11.got_ref.before_ref, bf16[2,128,128]{2,1,0:T(8,128)(2,1)S(1)} %get-tuple-element.23.get_ref, bf16[2,128,128]{2,1,0:T(8,128)(2,1)S(1)} %get-tuple-element.24.put_ref, ...), custom_call_target="tpu_custom_call" | custom-call | flops 268435456 | bytes 4194304 | tf_op jit(solution)/shard_map/pallas_call | solution.py:419
  43.4 0.1 copy.12
  43.5 13.2 %all_to_all.27 = bf16[2,128,128]{2,0,1:T(2,128)(2,1)S(1)} all-to-all(bf16[2,128,128]{2,0,1:T(2,128)(2,1)S(1)} %copy.12), channel_id=1, replica_groups=mesh['det'=4,'tm_0'=4,'tm_1'=4,'tm_2'=2] {'tm_2','tm_1','tm_0','det'}, dimensions={1} | all-to-all | bytes 131072 | tf_op jit(solution)/shard_map/all_to_all | solution.py:443
  56.7 0.0 copy-done
  56.7 0.6 shard_map.80
  57.3 0.1 copy.15
  57.3 13.8 %all_to_all.28 = bf16[3,128,128]{2,0,1:T(4,128)(2,1)S(1)} all-to-all(bf16[3,128,128]{2,0,1:T(4,128)(2,1)S(1)} %copy.15), channel_id=1, replica_groups=mesh['det'=4,'tm_0'=4,'tm_1'=4,'tm_2'=2] {'tm_2','tm_1','tm_0','det'}, dimensions={1} | all-to-all | bytes 196608 | tf_op jit(solution)/shard_map/all_to_all | solution.py:443
  71.2 1.6 %shard_map.81 = (bf16[3,128,128]{2,1,0:T(8,128)(2,1)S(1)}, f32[128,128]{1,0:T(8,128)S(1)}, f32[128,128]{1,0:T(8,128)S(1)}, f32[1,128]{1,0:T(1,128)S(1)}) custom-call(bf16[3,128,128]{2,1,0:T(8,128)(2,1)S(1)} %copy.16.got_ref, bf16[2,128,128]{2,1,0:T(8,128)(2,1)S(1)} %get-tuple-element.23.get_ref, bf16[2,128,128]{2,1,0:T(8,128)(2,1)S(1)} %get-tuple-element.24.put_ref, ...), custom_call_target="tpu_custom_call" | custom-call | flops 268435456 | bytes 4194304 | tf_op jit(solution)/shard_map/pallas_call | solution.py:419
  72.8 0.1 copy.17
  72.9 13.7 %all_to_all.29 = bf16[3,128,128]{2,0,1:T(4,128)(2,1)S(1)} all-to-all(bf16[3,128,128]{2,0,1:T(4,128)(2,1)S(1)} %copy.17), channel_id=1, replica_groups=mesh['det'=4,'tm_0'=4,'tm_1'=4,'tm_2'=2] {'tm_2','tm_1','tm_0','det'}, dimensions={1} | all-to-all | bytes 196608 | tf_op jit(solution)/shard_map/all_to_all | solution.py:443
  86.6 0.8 shard_map.82
  (5 shorter events, 0.1 us)
Async XLA Ops:
  0.6 56.0 %copy-start = (s32[16,2]{0,1:T(2,128)S(1)}, s32[16,2]{0,1:T(2,128)}, u32[]{:S(2)}) copy-start(s32[16,2]{0,1:T(2,128)} %param.11) | copy-start | bytes 388

commit v5 on v4

--- a/solution.py
+++ b/solution.py
@@ -56,7 +56,7 @@
 
 def _rotate(x, amount):
     step = 1
-    for base in (8, 4, 4):
+    for base in (16, 8):
         digit = (amount >> (step.bit_length() - 1)) & (base - 1)
         turned = x
         for value in range(1, base):
@@ -211,16 +211,16 @@
 
 def take_reply(got, get, shift):
     turned = _dot(get[0], got[0]) + _dot(get[1], got[1])
-    return _rotate(turned, (L - shift) & 127)
+    return _rotate(turned.astype(BF16), ((L - shift) & 127).astype(jnp.int16)).astype(F32)
 
 
 def send_back(back, put, shift):
-    turned = _rotate(back, shift).astype(BF16)
+    turned = _rotate(back.astype(BF16), shift.astype(jnp.int16))
     return [_dot(put[j], turned).astype(BF16) for j in range(2)]
 
 
 CHUNK = 16
-STEPS = (32, 32, 32, 32)
+STEPS = (32, 48, 48)
 DEPTH = 2
 
 

time: 87.7 us -> 87.3 us (level)
  no operation moved by 1% of the time
where the time goes in v5:
time: 87.3 us; the launch traced here: 87.1 us
  blocking collectives  75.7 us (87%)
  Pallas kernels  10.2 us (12%)
    all_to_all x5, blocking collectives, exchange(): return lax.all_to_all(x, SEND, split_axis=1, concat_axis=1, tiled=True)  75.7 us
    pallas_call x6, Pallas kernels, call(): pl.pallas_call(kernel, grid=grid, in_specs=in_specs, out_specs=out_specs,...  10.2 us

profile of v5, /device:TPU:1, one launch (start us, length us, event | category | flops | bytes accessed | tf_op | source)
XLA Modules:
  0.0 87.1 jit_solution(12412305699831296244)
XLA Ops:
  0.6 0.0 copy-start
  0.6 5.3 %shard_map.77 = (bf16[3,128,128]{2,1,0:T(8,128)(2,1)S(1)}, bf16[32,256,256]{2,1,0:T(8,128)(2,1)S(1)}, bf16[2,128,128]{2,1,0:T(8,128)(2,1)S(1)}, bf16[2,128,128]{2,1,0:T(8,128)(2,1)S(1)}, s32[128,128]{1,0:T(8,128)S(1)}) custom-call(s32[2,64]{1,0:T(2,128)} %tile_hbm.1, s32[2,64]{1,0:T(2,128)} %offset_hbm.1, bf16[128,256]{1,0:T(8,128)(2,1)} %bitcast.8, ...), custom_call_target="tpu_custom_call" | custom-call | flops 1073741824 | bytes 8388608 | tf_op jit(solution)/shard_map/pallas_call | solution.py:419
  6.0 0.1 copy.8
  6.1 21.3 %all_to_all.25 = bf16[3,128,128]{2,0,1:T(4,128)(2,1)S(1)} all-to-all(bf16[3,128,128]{2,0,1:T(4,128)(2,1)S(1)} %copy.8), channel_id=1, replica_groups=mesh['det'=4,'tm_0'=4,'tm_1'=4,'tm_2'=2] {'tm_2','tm_1','tm_0','det'}, dimensions={1} | all-to-all | bytes 196608 | tf_op jit(solution)/shard_map/all_to_all | solution.py:443
  27.4 0.5 shard_map.78
  27.9 0.1 copy.10
  28.0 13.7 %all_to_all.26 = bf16[3,128,128]{2,0,1:T(4,128)(2,1)S(1)} all-to-all(bf16[3,128,128]{2,0,1:T(4,128)(2,1)S(1)} %copy.10), channel_id=1, replica_groups=mesh['det'=4,'tm_0'=4,'tm_1'=4,'tm_2'=2] {'tm_2','tm_1','tm_0','det'}, dimensions={1} | all-to-all | bytes 196608 | tf_op jit(solution)/shard_map/all_to_all | solution.py:443
  41.7 1.4 %shard_map.79 = (bf16[2,128,128]{2,1,0:T(8,128)(2,1)S(1)}, f32[128,128]{1,0:T(8,128)S(1)}) custom-call(bf16[3,128,128]{2,1,0:T(8,128)(2,1)S(1)} %copy.11.got_ref.before_ref, bf16[2,128,128]{2,1,0:T(8,128)(2,1)S(1)} %get-tuple-element.23.get_ref, bf16[2,128,128]{2,1,0:T(8,128)(2,1)S(1)} %get-tuple-element.24.put_ref, ...), custom_call_target="tpu_custom_call" | custom-call | flops 268435456 | bytes 4194304 | tf_op jit(solution)/shard_map/pallas_call | solution.py:419
  43.1 0.1 copy.12
  43.2 13.2 %all_to_all.27 = bf16[2,128,128]{2,0,1:T(2,128)(2,1)S(1)} all-to-all(bf16[2,128,128]{2,0,1:T(2,128)(2,1)S(1)} %copy.12), channel_id=1, replica_groups=mesh['det'=4,'tm_0'=4,'tm_1'=4,'tm_2'=2] {'tm_2','tm_1','tm_0','det'}, dimensions={1} | all-to-all | bytes 131072 | tf_op jit(solution)/shard_map/all_to_all | solution.py:443
  56.4 0.0 copy-done
  56.4 0.6 shard_map.80
  57.0 0.1 copy.15
  57.1 13.8 %all_to_all.28 = bf16[3,128,128]{2,0,1:T(4,128)(2,1)S(1)} all-to-all(bf16[3,128,128]{2,0,1:T(4,128)(2,1)S(1)} %copy.15), channel_id=1, replica_groups=mesh['det'=4,'tm_0'=4,'tm_1'=4,'tm_2'=2] {'tm_2','tm_1','tm_0','det'}, dimensions={1} | all-to-all | bytes 196608 | tf_op jit(solution)/shard_map/all_to_all | solution.py:443
  70.9 1.6 %shard_map.81 = (bf16[3,128,128]{2,1,0:T(8,128)(2,1)S(1)}, f32[128,128]{1,0:T(8,128)S(1)}, f32[128,128]{1,0:T(8,128)S(1)}, f32[1,128]{1,0:T(1,128)S(1)}) custom-call(bf16[3,128,128]{2,1,0:T(8,128)(2,1)S(1)} %copy.16.got_ref, bf16[2,128,128]{2,1,0:T(8,128)(2,1)S(1)} %get-tuple-element.23.get_ref, bf16[2,128,128]{2,1,0:T(8,128)(2,1)S(1)} %get-tuple-element.24.put_ref, ...), custom_call_target="tpu_custom_call" | custom-call | flops 268435456 | bytes 4194304 | tf_op jit(solution)/shard_map/pallas_call | solution.py:419
  72.5 0.1 copy.17
  72.6 13.7 %all_to_all.29 = bf16[3,128,128]{2,0,1:T(4,128)(2,1)S(1)} all-to-all(bf16[3,128,128]{2,0,1:T(4,128)(2,1)S(1)} %copy.17), channel_id=1, replica_groups=mesh['det'=4,'tm_0'=4,'tm_1'=4,'tm_2'=2] {'tm_2','tm_1','tm_0','det'}, dimensions={1} | all-to-all | bytes 196608 | tf_op jit(solution)/shard_map/all_to_all | solution.py:443
  86.2 0.8 shard_map.82
  (5 shorter events, 0.1 us)
Async XLA Ops:
  0.6 55.7 %copy-start = (s32[16,2]{0,1:T(2,128)S(1)}, s32[16,2]{0,1:T(2,128)}, u32[]{:S(2)}) copy-start(s32[16,2]{0,1:T(2,128)} %param.11) | copy-start | bytes 388

commit v6 on v5

--- a/solution.py
+++ b/solution.py
@@ -56,7 +56,7 @@
 
 def _rotate(x, amount):
     step = 1
-    for base in (16, 8):
+    for base in (8, 4, 4):
         digit = (amount >> (step.bit_length() - 1)) & (base - 1)
         turned = x
         for value in range(1, base):
@@ -324,7 +324,7 @@
 
 
 def first_apply_kernel(
-    got_ref, get_ref, put_ref, shift_ref, normal_ref, message_ref, foot_ref, back
+    got_ref, get_ref, put_ref, shift_ref, normal_ref, field_ref, neighbour_ref, message_ref, foot_ref, prior_ref, back
 ):
     shift = shift_ref[...]
     foot = take_reply((got_ref[0], got_ref[1]), (get_ref[0], get_ref[1]), shift)
@@ -334,18 +334,17 @@
     )
     message_ref[0] = parts[0]
     message_ref[1] = parts[1]
-
-
-def middle_kernel(got_ref, before_ref, field_ref, neighbour_ref, pick_ref, place_ref, shift_ref, image_ref, prior_ref, message_ref):
+    before, after = outer_edges(got_ref[2], neighbour_ref[...])
+    prior_ref[...] = prior(field_ref[...], before, after)
+
+
+def middle_kernel(got_ref, field_ref, smooth_ref, pick_ref, place_ref, shift_ref, image_ref, message_ref):
     field = field_ref[...]
     pick = [pick_ref[k] for k in range(4)]
     place = [place_ref[k] for k in range(4)]
     shifts = [shift_ref[j] for j in range(2)]
-    before, after = outer_edges(before_ref[2], neighbour_ref[...])
-    smooth = prior(field, before, after)
-    image = add_up((got_ref[0], got_ref[1]), place, shifts) + smooth
+    image = add_up((got_ref[0], got_ref[1]), place, shifts) + smooth_ref[...]
     replies = reply(image, pick, shifts)
-    prior_ref[...] = smooth
     image_ref[...] = image
     message_ref[0] = replies[0]
     message_ref[1] = replies[1]
@@ -488,22 +487,22 @@
         [WIDE, _shape((3, L, L), BF16), _shape((4, L, L), BF16), _shape((4, L, L), BF16), _shape((2, L, L), jnp.int32)],
         (got,),
     )
-    got_first = exchange(message)
-
-    message, foot = whole_call(
+    got = exchange(message)
+
+    message, foot, smooth = whole_call(
         first_apply_kernel,
-        [_shape((2, L, L), BF16), WIDE],
-        (got_first, get, put, shift, normal),
+        [_shape((2, L, L), BF16), WIDE, WIDE],
+        (got, get, put, shift, normal, field, neighbours),
         [pltpu.VMEM(MAP, F32)],
         2**28,
         2**22,
     )
     got = exchange(message)
 
-    image, smooth, message = whole_call(
+    image, message = whole_call(
         middle_kernel,
-        [WIDE, WIDE, _shape((3, L, L), BF16)],
-        (got, got_first, field, neighbours, pick, place, shifts),
+        [WIDE, _shape((3, L, L), BF16)],
+        (got, field, smooth, pick, place, shifts),
     )
     got = exchange(message)
 

time: 87.3 us -> 87.3 us (level)
  no operation moved by 1% of the time
where the time goes in v6:
time: 87.3 us; the launch traced here: 87.1 us
  blocking collectives  75.7 us (87%)
  Pallas kernels  10.2 us (12%)
    all_to_all x5, blocking collectives, exchange(): return lax.all_to_all(x, SEND, split_axis=1, concat_axis=1, tiled=True)  75.7 us
    pallas_call x6, Pallas kernels, call(): pl.pallas_call(kernel, grid=grid, in_specs=in_specs, out_specs=out_specs,...  10.2 us

profile of v6, /device:TPU:1, one launch (start us, length us, event | category | flops | bytes accessed | tf_op | source)
XLA Modules:
  0.0 87.1 jit_solution(7526806595025783791)
XLA Ops:
  0.6 0.0 copy-start
  0.6 5.4 %shard_map.77 = (bf16[3,128,128]{2,1,0:T(8,128)(2,1)S(1)}, bf16[32,256,256]{2,1,0:T(8,128)(2,1)S(1)}, bf16[2,128,128]{2,1,0:T(8,128)(2,1)S(1)}, bf16[2,128,128]{2,1,0:T(8,128)(2,1)S(1)}, s32[128,128]{1,0:T(8,128)S(1)}) custom-call(s32[2,64]{1,0:T(2,128)} %tile_hbm.1, s32[2,64]{1,0:T(2,128)} %offset_hbm.1, bf16[128,256]{1,0:T(8,128)(2,1)} %bitcast.8, ...), custom_call_target="tpu_custom_call" | custom-call | flops 1073741824 | bytes 8388608 | tf_op jit(solution)/shard_map/pallas_call | solution.py:418
  6.0 0.1 copy.8
  6.1 21.3 %all_to_all.25 = bf16[3,128,128]{2,0,1:T(4,128)(2,1)S(1)} all-to-all(bf16[3,128,128]{2,0,1:T(4,128)(2,1)S(1)} %copy.8), channel_id=1, replica_groups=mesh['det'=4,'tm_0'=4,'tm_1'=4,'tm_2'=2] {'tm_2','tm_1','tm_0','det'}, dimensions={1} | all-to-all | bytes 196608 | tf_op jit(solution)/shard_map/all_to_all | solution.py:442
  27.4 0.5 shard_map.78
  27.9 0.1 copy.10
  28.0 13.7 %all_to_all.26 = bf16[3,128,128]{2,0,1:T(4,128)(2,1)S(1)} all-to-all(bf16[3,128,128]{2,0,1:T(4,128)(2,1)S(1)} %copy.10), channel_id=1, replica_groups=mesh['det'=4,'tm_0'=4,'tm_1'=4,'tm_2'=2] {'tm_2','tm_1','tm_0','det'}, dimensions={1} | all-to-all | bytes 196608 | tf_op jit(solution)/shard_map/all_to_all | solution.py:442
  41.7 0.0 copy-done
  41.7 1.6 %shard_map.79 = (bf16[2,128,128]{2,1,0:T(8,128)(2,1)S(1)}, f32[128,128]{1,0:T(8,128)S(1)}, f32[128,128]{1,0:T(8,128)S(1)}) custom-call(bf16[3,128,128]{2,1,0:T(8,128)(2,1)S(1)} %copy.11.got_ref, bf16[2,128,128]{2,1,0:T(8,128)(2,1)S(1)} %get-tuple-element.23.get_ref, bf16[2,128,128]{2,1,0:T(8,128)(2,1)S(1)} %get-tuple-element.24.put_ref, ...), custom_call_target="tpu_custom_call" | custom-call | flops 268435456 | bytes 4194304 | tf_op jit(solution)/shard_map/pallas_call | solution.py:418
  43.3 0.1 copy.12
  43.4 13.2 %all_to_all.27 = bf16[2,128,128]{2,0,1:T(2,128)(2,1)S(1)} all-to-all(bf16[2,128,128]{2,0,1:T(2,128)(2,1)S(1)} %copy.12), channel_id=1, replica_groups=mesh['det'=4,'tm_0'=4,'tm_1'=4,'tm_2'=2] {'tm_2','tm_1','tm_0','det'}, dimensions={1} | all-to-all | bytes 131072 | tf_op jit(solution)/shard_map/all_to_all | solution.py:442
  56.6 0.4 shard_map.80
  57.0 0.1 copy.14
  57.1 13.8 %all_to_all.28 = bf16[3,128,128]{2,0,1:T(4,128)(2,1)S(1)} all-to-all(bf16[3,128,128]{2,0,1:T(4,128)(2,1)S(1)} %copy.14), channel_id=1, replica_groups=mesh['det'=4,'tm_0'=4,'tm_1'=4,'tm_2'=2] {'tm_2','tm_1','tm_0','det'}, dimensions={1} | all-to-all | bytes 196608 | tf_op jit(solution)/shard_map/all_to_all | solution.py:442
  71.0 1.5 %shard_map.81 = (bf16[3,128,128]{2,1,0:T(8,128)(2,1)S(1)}, f32[128,128]{1,0:T(8,128)S(1)}, f32[128,128]{1,0:T(8,128)S(1)}, f32[1,128]{1,0:T(1,128)S(1)}) custom-call(bf16[3,128,128]{2,1,0:T(8,128)(2,1)S(1)} %copy.15.got_ref, bf16[2,128,128]{2,1,0:T(8,128)(2,1)S(1)} %get-tuple-element.23.get_ref, bf16[2,128,128]{2,1,0:T(8,128)(2,1)S(1)} %get-tuple-element.24.put_ref, ...), custom_call_target="tpu_custom_call" | custom-call | flops 268435456 | bytes 4194304 | tf_op jit(solution)/shard_map/pallas_call | solution.py:418
  72.5 0.1 copy.16
  72.6 13.7 %all_to_all.29 = bf16[3,128,128]{2,0,1:T(4,128)(2,1)S(1)} all-to-all(bf16[3,128,128]{2,0,1:T(4,128)(2,1)S(1)} %copy.16), channel_id=1, replica_groups=mesh['det'=4,'tm_0'=4,'tm_1'=4,'tm_2'=2] {'tm_2','tm_1','tm_0','det'}, dimensions={1} | all-to-all | bytes 196608 | tf_op jit(solution)/shard_map/all_to_all | solution.py:442
  86.3 0.8 shard_map.82
  (5 shorter events, 0.1 us)
Async XLA Ops:
  0.6 41.1 %copy-start = (s32[16,2]{0,1:T(2,128)S(1)}, s32[16,2]{0,1:T(2,128)}, u32[]{:S(2)}) copy-start(s32[16,2]{0,1:T(2,128)} %param.11) | copy-start | bytes 388

commit v7 on v6

--- a/solution.py
+++ b/solution.py
@@ -99,12 +99,12 @@
     return (tm_2 << 6) | (tm_1 << 4) | (tm_0 << 2) | det
 
 
-def _blocks_of(owner_row, j):
-    block = _iota((L, L), 1)
-    return _onehot((_iota((L, L), 0) == owner_row) & ((block & 1) == j))
-
-
-def places(tile_row, offset_row, put):
+def _blocks_of(owner_row, rows):
+    line = _iota((L * rows, L), 0)
+    return _onehot(line == owner_row * rows + (_iota((L * rows, L), 1) & 1))
+
+
+def places(tile_row, offset_row):
     tile = tile_row.astype(jnp.int32)
     offset = offset_row.astype(jnp.int32)
     start_row = (offset >> 7) * ROW_STEP + (tile & 15)
@@ -115,7 +115,8 @@
         start_row.astype(F32),
         jnp.where(line == place + 1, (offset & 127).astype(F32), 0.0),
     ).astype(BF16)
-    return _dot_nt(put[0] + put[1], facts).astype(BF16)
+    third = _onehot(_iota((4 * L, L), 0) == _owner(tile) * 4 + 2)
+    return _dot_nt(third, facts)
 
 
 def block_tables(tile_row, offset_row):
@@ -126,8 +127,7 @@
     block = _iota((L, L), 0)
     device = _iota((L, L), 1)
     get = [_onehot((device == owner_col) & ((block & 1) == j)) for j in range(2)]
-    put = [_blocks_of(owner, j) for j in range(2)]
-    return get, put, jnp.broadcast_to(shift_col, (L, L))
+    return get, _blocks_of(owner, 2), _blocks_of(owner, 4), jnp.broadcast_to(shift_col, (L, L))
 
 
 def owner_tables(facts):
@@ -216,7 +216,7 @@
 
 def send_back(back, put, shift):
     turned = _rotate(back.astype(BF16), shift.astype(jnp.int16))
-    return [_dot(put[j], turned).astype(BF16) for j in range(2)]
+    return _dot(put, turned)
 
 
 CHUNK = 16
@@ -226,8 +226,8 @@
 
 def rhs_kernel(
     tile_hbm, offset_hbm, tod_hbm, weight_hbm, beam_hbm,
-    message_ref, normal_ref, get_ref, put_ref, shift_ref,
-    tile_ref, offset_ref, tod_ref, weight_ref, beam_ref, weighted, back, scratch, small_sems, sems,
+    message_ref, normal_ref, get_ref, put_2_ref, put_4_ref, shift_ref,
+    tile_ref, offset_ref, tod_ref, weight_ref, beam_ref, weighted, back, scratch, facts, small_sems, sems,
 ):
     small = [
         pltpu.make_async_copy(src, dst, small_sems.at[k])
@@ -256,12 +256,13 @@
     small[1].wait()
     tile_row = _as_row(tile_ref[...], scratch)
     offset_row = _as_row(offset_ref[...], scratch)
-    get, put, shift = block_tables(tile_row, offset_row)
+    get, put_2, put_4, shift = block_tables(tile_row, offset_row)
     for j in range(2):
         get_ref[j] = get[j]
-        put_ref[j] = put[j]
+    put_2_ref[...] = put_2
+    put_4_ref[...] = put_4
     shift_ref[...] = shift
-    message_ref[2] = places(tile_row, offset_row, put)
+    facts[...] = places(tile_row, offset_row)
     small[2].wait()
     small[3].wait()
     weighted[...] = (weight_ref[...] * tod_ref[...].astype(F32)).astype(BF16)
@@ -286,9 +287,7 @@
                 out = jnp.where(row == k, found[FOOT:], out)
             back[first : first + CHUNK] = out
 
-    parts = send_back(back[...], put, shift)
-    message_ref[0] = parts[0]
-    message_ref[1] = parts[1]
+    message_ref[...] = (facts[...] + send_back(back[...], put_4_ref[...], shift_ref[...])).astype(BF16)
 
 
 def apply_normal(normal_ref, foot, back):
@@ -329,11 +328,8 @@
     shift = shift_ref[...]
     foot = take_reply((got_ref[0], got_ref[1]), (get_ref[0], get_ref[1]), shift)
     foot_ref[...] = foot
-    parts = send_back(
-        apply_normal(normal_ref, foot, back), (put_ref[0], put_ref[1]), shift
-    )
-    message_ref[0] = parts[0]
-    message_ref[1] = parts[1]
+    turned = apply_normal(normal_ref, foot, back)
+    message_ref[...] = send_back(turned, put_ref[...], shift).astype(BF16)
     before, after = outer_edges(got_ref[2], neighbour_ref[...])
     prior_ref[...] = prior(field_ref[...], before, after)
 
@@ -373,13 +369,11 @@
     residual_ref[...] = residual
     prior_ref[...] = smooth
     turned = apply_normal(normal_ref, foot, back)
-    parts = send_back(turned, (put_ref[0], put_ref[1]), shift)
-    message_ref[0] = parts[0]
-    message_ref[1] = parts[1]
     square = _total(residual * residual)
     product = _total(foot * turned + residual * smooth)
     extra = _pieces(square, SCALARS) + _pieces(product, SCALARS + 3)
-    message_ref[2] = jnp.broadcast_to(extra, (L, L)).astype(BF16)
+    third = (_iota((4 * L, L), 0) & 3) == 2
+    message_ref[...] = jnp.where(third, extra, send_back(turned, put_ref[...], shift)).astype(BF16)
 
 
 def last_kernel(got_ref, place_ref, shift_ref, field_ref, image_ref, residual_ref, smooth_ref, sums_ref, solution_ref, rest_ref):
@@ -442,21 +436,27 @@
     return lax.all_to_all(x, SEND, split_axis=1, concat_axis=1, tiled=True)
 
 
+def exchange_rows(x):
+    x = lax.all_to_all(x.reshape(L, -1, L), SEND, split_axis=0, concat_axis=0, tiled=True)
+    return x.transpose(1, 0, 2)
+
+
 def per_device(tod, pointing, weights, tile_ids, offsets, neighbours):
     neighbours = neighbours.T
 
-    message, normal, get, put, shift = call(
+    message, normal, get, put_2, put_4, shift = call(
         rhs_kernel,
         (),
         [pl.BlockSpec(memory_space=pltpu.HBM)] * 5,
         [
-            _shape((3, L, L), BF16),
+            _shape((4 * L, L), BF16),
             pltpu.VMEM((L // 4, 2 * FOOT, 2 * FOOT), BF16),
             _shape((2, L, L), BF16),
-            _shape((2, L, L), BF16),
+            _shape((2 * L, L), BF16),
+            _shape((4 * L, L), BF16),
             _shape((L, L), jnp.int32),
         ],
-        [pl.BlockSpec(memory_space=pltpu.VMEM)] * 5,
+        [pl.BlockSpec(memory_space=pltpu.VMEM)] * 6,
         [
             pltpu.VMEM(tile_ids.shape, jnp.int32),
             pltpu.VMEM(offsets.shape, jnp.int32),
@@ -466,6 +466,7 @@
             pltpu.VMEM((L, SAMP), BF16),
             pltpu.VMEM((L, FOOT), F32),
             pltpu.VMEM((8, L), F32),
+            pltpu.VMEM((4 * L, L), F32),
             pltpu.SemaphoreType.DMA((4,)),
             pltpu.SemaphoreType.DMA((len(STEPS),)),
         ],
@@ -480,7 +481,7 @@
         2**23,
         16,
     )
-    got = exchange(message)
+    got = exchange_rows(message)
 
     field, message, pick, place, shifts = whole_call(
         start_kernel,
@@ -491,13 +492,13 @@
 
     message, foot, smooth = whole_call(
         first_apply_kernel,
-        [_shape((2, L, L), BF16), WIDE, WIDE],
-        (got, get, put, shift, normal, field, neighbours),
+        [_shape((2 * L, L), BF16), WIDE, WIDE],
+        (got, get, put_2, shift, normal, field, neighbours),
         [pltpu.VMEM(MAP, F32)],
         2**28,
         2**22,
     )
-    got = exchange(message)
+    got = exchange_rows(message)
 
     image, message = whole_call(
         middle_kernel,
@@ -508,13 +509,13 @@
 
     message, residual, smooth, sums = whole_call(
         second_apply_kernel,
-        [_shape((3, L, L), BF16), WIDE, WIDE, _shape((1, L), F32)],
-        (got, get, put, shift, normal, foot, field, image, smooth, neighbours),
+        [_shape((4 * L, L), BF16), WIDE, WIDE, _shape((1, L), F32)],
+        (got, get, put_4, shift, normal, foot, field, image, smooth, neighbours),
         [pltpu.VMEM(MAP, F32)],
         2**28,
         2**22,
     )
-    got = exchange(message)
+    got = exchange_rows(message)
 
     return tuple(
         whole_call(

time: 87.3 us -> 87.2 us (level)
    all_to_all x5 -> x2, blocking collectives: 75.7 us -> 27.5 us  [exchange(): return lax.all_to_all(x, SEND, split_axis=1, concat_axis=1, tiled=True)]
    all_to_all x0 -> x3, blocking collectives: none -> 48.2 us  [exchange_rows(): lax.all_to_all(x.reshape(L, -1, L), SEND, split_axis=0, concat_axis=0, ti...]
where the time goes in v7:
time: 87.2 us; the launch traced here: 87 us
  blocking collectives  75.7 us (87%)
  Pallas kernels  10.3 us (12%)
    all_to_all x3, blocking collectives, exchange_rows(): lax.all_to_all(x.reshape(L, -1, L), SEND, split_axis=0, concat_axis=0, ti...  48.2 us
    all_to_all x2, blocking collectives, exchange(): return lax.all_to_all(x, SEND, split_axis=1, concat_axis=1, tiled=True)  27.5 us
    pallas_call x6, Pallas kernels, call(): pl.pallas_call(kernel, grid=grid, in_specs=in_specs, out_specs=out_specs,...  10.3 us

profile of v7, /device:TPU:1, one launch (start us, length us, event | category | flops | bytes accessed | tf_op | source)
XLA Modules:
  0.0 87.0 jit_solution(1595130095230672797)
XLA Ops:
  0.6 0.0 copy-start
  0.6 5.4 %shard_map.77 = (bf16[512,128]{1,0:T(8,128)(2,1)S(1)}, bf16[32,256,256]{2,1,0:T(8,128)(2,1)S(1)}, bf16[2,128,128]{2,1,0:T(8,128)(2,1)S(1)}, bf16[256,128]{1,0:T(...) custom-call(s32[2,64]{1,0:T(2,128)} %tile_hbm.1, s32[2,64]{1,0:T(2,128)} %offset_hbm.1, ...), custom_call_target="tpu_custom_call" | custom-call | flops 1073741824 | bytes 8388608 | tf_op jit(solution)/shard_map/pallas_call | solution.py:412
  6.0 21.3 %all_to_all.25 = bf16[128,4,128]{2,1,0:T(4,128)(2,1)S(1)} all-to-all(bf16[128,4,128]{2,1,0:T(4,128)(2,1)S(1)} %bitcast.20), channel_id=1, replica_groups=mesh['det'=4,'tm_0'=4,'tm_1'=4,'tm_2'=2] {'tm_2','tm_1','tm_0','det'}, dimensions={0} | all-to-all | bytes 262144 | tf_op jit(solution)/shard_map/all_to_all | solution.py:440
  27.4 0.5 shard_map.78
  27.9 0.1 copy.12
  28.0 13.7 %all_to_all.26 = bf16[3,128,128]{2,0,1:T(4,128)(2,1)S(1)} all-to-all(bf16[3,128,128]{2,0,1:T(4,128)(2,1)S(1)} %copy.12), channel_id=1, replica_groups=mesh['det'=4,'tm_0'=4,'tm_1'=4,'tm_2'=2] {'tm_2','tm_1','tm_0','det'}, dimensions={1} | all-to-all | bytes 196608 | tf_op jit(solution)/shard_map/all_to_all | solution.py:436
  41.6 0.0 copy-done
  41.7 1.6 %shard_map.79 = (bf16[256,128]{1,0:T(8,128)(2,1)S(1)}, f32[128,128]{1,0:T(8,128)S(1)}, f32[128,128]{1,0:T(8,128)S(1)}) custom-call(bf16[3,128,128]{2,1,0:T(8,128)(2,1)S(1)} %copy.13.got_ref, bf16[2,128,128]{2,1,0:T(8,128)(2,1)S(1)} %get-tuple-element.24.get_ref, bf16[256,128]{1,0:T(8,128)(2,1)S(1)} %get-tuple-element.25.put_ref, ...), custom_call_target="tpu_custom_call" | custom-call | flops 268435456 | bytes 4194304 | tf_op jit(solution)/shard_map/pallas_call | solution.py:412
  43.3 13.2 %all_to_all.27 = bf16[128,2,128]{2,1,0:T(2,128)(2,1)S(1)} all-to-all(bf16[128,2,128]{2,1,0:T(2,128)(2,1)S(1)} %bitcast.21), channel_id=1, replica_groups=mesh['det'=4,'tm_0'=4,'tm_1'=4,'tm_2'=2] {'tm_2','tm_1','tm_0','det'}, dimensions={0} | all-to-all | bytes 131072 | tf_op jit(solution)/shard_map/all_to_all | solution.py:440
  56.5 0.4 shard_map.80
  56.9 0.1 copy.15
  57.0 13.8 %all_to_all.28 = bf16[3,128,128]{2,0,1:T(4,128)(2,1)S(1)} all-to-all(bf16[3,128,128]{2,0,1:T(4,128)(2,1)S(1)} %copy.15), channel_id=1, replica_groups=mesh['det'=4,'tm_0'=4,'tm_1'=4,'tm_2'=2] {'tm_2','tm_1','tm_0','det'}, dimensions={1} | all-to-all | bytes 196608 | tf_op jit(solution)/shard_map/all_to_all | solution.py:436
  70.8 1.6 %shard_map.81 = (bf16[512,128]{1,0:T(8,128)(2,1)S(1)}, f32[128,128]{1,0:T(8,128)S(1)}, f32[128,128]{1,0:T(8,128)S(1)}, f32[1,128]{1,0:T(1,128)S(1)}) custom-call(bf16[3,128,128]{2,1,0:T(8,128)(2,1)S(1)} %copy.16.got_ref, bf16[2,128,128]{2,1,0:T(8,128)(2,1)S(1)} %get-tuple-element.24.get_ref, bf16[512,128]{1,0:T(8,128)(2,1)S(1)} %get-tuple-element.35.put_ref, ...), custom_call_target="tpu_custom_call" | custom-call | flops 268435456 | bytes 4194304 | tf_op jit(solution)/shard_map/pallas_call | solution.py:412
  72.5 13.7 %all_to_all.29 = bf16[128,4,128]{2,1,0:T(4,128)(2,1)S(1)} all-to-all(bf16[128,4,128]{2,1,0:T(4,128)(2,1)S(1)} %bitcast.19), channel_id=1, replica_groups=mesh['det'=4,'tm_0'=4,'tm_1'=4,'tm_2'=2] {'tm_2','tm_1','tm_0','det'}, dimensions={0} | all-to-all | bytes 262144 | tf_op jit(solution)/shard_map/all_to_all | solution.py:440
  86.1 0.8 shard_map.82
  (5 shorter events, 0.1 us)
Async XLA Ops:
  0.6 41.0 %copy-start = (s32[16,2]{0,1:T(2,128)S(1)}, s32[16,2]{0,1:T(2,128)}, u32[]{:S(2)}) copy-start(s32[16,2]{0,1:T(2,128)} %param.11) | copy-start | bytes 388

commit v8 on v7

--- a/solution.py
+++ b/solution.py
@@ -196,14 +196,11 @@
 
 def prior(field, before, after):
     lane = _iota((L, L), 1)
-    row = _iota((L, L), 0)
     to_right = _roll(field, 1, 1)
     to_left = _roll(field, L - 1, 1)
-    left_in = _roll(to_right, ROW_STEP, 0)
-    right_in = _roll(to_left, L - ROW_STEP, 0)
-    pad = jnp.zeros((L - TILE, 1), F32)
-    left_in = jnp.where(row < TILE, jnp.concatenate([before, pad], axis=0), left_in)
-    right_in = jnp.where(row >= L - TILE, jnp.concatenate([pad, after], axis=0), right_in)
+    edge = (TILE, L)
+    left_in = jnp.concatenate([jnp.broadcast_to(before, edge), to_right[: L - TILE]], axis=0)
+    right_in = jnp.concatenate([to_left[TILE:], jnp.broadcast_to(after, edge)], axis=0)
     lefts = jnp.where(lane == 0, left_in, to_right)
     rights = jnp.where(lane == L - 1, right_in, to_left)
     return smooth_weight * (2.0 * field - lefts - rights) + ridge_weight * field
@@ -388,7 +385,7 @@
     step_first = norm_first / _whole(sums, SCALARS + 3)
     norm = _whole(more, SCALARS)
     ratio = norm / norm_first
-    step = norm / (_whole(more, SCALARS + 3) - ratio * norm / step_first)
+    step = norm / (_whole(more, SCALARS + 3) - ratio * (norm / step_first))
     solution = step_first * field + step * (residual + ratio * field)
     rest = residual - step * (image + ratio * image_ref[...])
     for q in range(8):

time: 87.2 us -> 87.1 us (level)
  no operation moved by 1% of the time
where the time goes in v8:
time: 87.1 us; the launch traced here: 86.9 us
  blocking collectives  75.7 us (87%)
  Pallas kernels  10.2 us (12%)
    all_to_all x3, blocking collectives, exchange_rows(): lax.all_to_all(x.reshape(L, -1, L), SEND, split_axis=0, concat_axis=0, ti...  48.2 us
    all_to_all x2, blocking collectives, exchange(): return lax.all_to_all(x, SEND, split_axis=1, concat_axis=1, tiled=True)  27.5 us
    pallas_call x6, Pallas kernels, call(): pl.pallas_call(kernel, grid=grid, in_specs=in_specs, out_specs=out_specs,...  10.2 us

profile of v8, /device:TPU:1, one launch (start us, length us, event | category | flops | bytes accessed | tf_op | source)
XLA Modules:
  0.0 86.9 jit_solution(1471371067174177018)
XLA Ops:
  0.6 0.0 copy-start
  0.6 5.4 %shard_map.77 = (bf16[512,128]{1,0:T(8,128)(2,1)S(1)}, bf16[32,256,256]{2,1,0:T(8,128)(2,1)S(1)}, bf16[2,128,128]{2,1,0:T(8,128)(2,1)S(1)}, bf16[256,128]{1,0:T(...) custom-call(s32[2,64]{1,0:T(2,128)} %tile_hbm.1, s32[2,64]{1,0:T(2,128)} %offset_hbm.1, ...), custom_call_target="tpu_custom_call" | custom-call | flops 1073741824 | bytes 8388608 | tf_op jit(solution)/shard_map/pallas_call | solution.py:409
  6.0 21.3 %all_to_all.25 = bf16[128,4,128]{2,1,0:T(4,128)(2,1)S(1)} all-to-all(bf16[128,4,128]{2,1,0:T(4,128)(2,1)S(1)} %bitcast.20), channel_id=1, replica_groups=mesh['det'=4,'tm_0'=4,'tm_1'=4,'tm_2'=2] {'tm_2','tm_1','tm_0','det'}, dimensions={0} | all-to-all | bytes 262144 | tf_op jit(solution)/shard_map/all_to_all | solution.py:437
  27.4 0.5 shard_map.78
  27.9 0.1 copy.12
  28.0 13.7 %all_to_all.26 = bf16[3,128,128]{2,0,1:T(4,128)(2,1)S(1)} all-to-all(bf16[3,128,128]{2,0,1:T(4,128)(2,1)S(1)} %copy.12), channel_id=1, replica_groups=mesh['det'=4,'tm_0'=4,'tm_1'=4,'tm_2'=2] {'tm_2','tm_1','tm_0','det'}, dimensions={1} | all-to-all | bytes 196608 | tf_op jit(solution)/shard_map/all_to_all | solution.py:433
  41.6 0.0 copy-done
  41.7 1.6 %shard_map.79 = (bf16[256,128]{1,0:T(8,128)(2,1)S(1)}, f32[128,128]{1,0:T(8,128)S(1)}, f32[128,128]{1,0:T(8,128)S(1)}) custom-call(bf16[3,128,128]{2,1,0:T(8,128)(2,1)S(1)} %copy.13.got_ref, bf16[2,128,128]{2,1,0:T(8,128)(2,1)S(1)} %get-tuple-element.24.get_ref, bf16[256,128]{1,0:T(8,128)(2,1)S(1)} %get-tuple-element.25.put_ref, ...), custom_call_target="tpu_custom_call" | custom-call | flops 268435456 | bytes 4194304 | tf_op jit(solution)/shard_map/pallas_call | solution.py:409
  43.2 13.2 %all_to_all.27 = bf16[128,2,128]{2,1,0:T(2,128)(2,1)S(1)} all-to-all(bf16[128,2,128]{2,1,0:T(2,128)(2,1)S(1)} %bitcast.21), channel_id=1, replica_groups=mesh['det'=4,'tm_0'=4,'tm_1'=4,'tm_2'=2] {'tm_2','tm_1','tm_0','det'}, dimensions={0} | all-to-all | bytes 131072 | tf_op jit(solution)/shard_map/all_to_all | solution.py:437
  56.4 0.4 shard_map.80
  56.8 0.1 copy.15
  56.9 13.8 %all_to_all.28 = bf16[3,128,128]{2,0,1:T(4,128)(2,1)S(1)} all-to-all(bf16[3,128,128]{2,0,1:T(4,128)(2,1)S(1)} %copy.15), channel_id=1, replica_groups=mesh['det'=4,'tm_0'=4,'tm_1'=4,'tm_2'=2] {'tm_2','tm_1','tm_0','det'}, dimensions={1} | all-to-all | bytes 196608 | tf_op jit(solution)/shard_map/all_to_all | solution.py:433
  70.8 1.6 %shard_map.81 = (bf16[512,128]{1,0:T(8,128)(2,1)S(1)}, f32[128,128]{1,0:T(8,128)S(1)}, f32[128,128]{1,0:T(8,128)S(1)}, f32[1,128]{1,0:T(1,128)S(1)}) custom-call(bf16[3,128,128]{2,1,0:T(8,128)(2,1)S(1)} %copy.16.got_ref, bf16[2,128,128]{2,1,0:T(8,128)(2,1)S(1)} %get-tuple-element.24.get_ref, bf16[512,128]{1,0:T(8,128)(2,1)S(1)} %get-tuple-element.35.put_ref, ...), custom_call_target="tpu_custom_call" | custom-call | flops 268435456 | bytes 4194304 | tf_op jit(solution)/shard_map/pallas_call | solution.py:409
  72.4 13.7 %all_to_all.29 = bf16[128,4,128]{2,1,0:T(4,128)(2,1)S(1)} all-to-all(bf16[128,4,128]{2,1,0:T(4,128)(2,1)S(1)} %bitcast.19), channel_id=1, replica_groups=mesh['det'=4,'tm_0'=4,'tm_1'=4,'tm_2'=2] {'tm_2','tm_1','tm_0','det'}, dimensions={0} | all-to-all | bytes 262144 | tf_op jit(solution)/shard_map/all_to_all | solution.py:437
  86.1 0.8 shard_map.82
  (5 shorter events, 0.1 us)
Async XLA Ops:
  0.6 41.0 %copy-start = (s32[16,2]{0,1:T(2,128)S(1)}, s32[16,2]{0,1:T(2,128)}, u32[]{:S(2)}) copy-start(s32[16,2]{0,1:T(2,128)} %param.11) | copy-start | bytes 388

commit v9 on v8

--- a/solution.py
+++ b/solution.py
@@ -140,27 +140,27 @@
             pick.append(_onehot(_iota((L, L), 1).astype(F32) == start_col + step))
             place.append(_onehot(_iota((L, L), 0).astype(F32) == start_row + step))
         shifts.append(jnp.broadcast_to(facts[:, 2 * j + 1 : 2 * j + 2], (L, L)).astype(jnp.int32))
-    return pick, place, shifts
+    return jnp.concatenate(pick, axis=0), jnp.concatenate(place, axis=1), shifts
 
 
 def add_up(got, place, shifts):
     lane = _iota((L, L), 1)
-    total = None
+    parts = []
     for j in range(2):
         x = got[j].astype(F32)
-        upper = jnp.where(lane >= shifts[j], x, 0.0).astype(BF16)
-        lower = jnp.where(lane < shifts[j], x, 0.0).astype(BF16)
-        part = _dot(place[2 * j], upper) + _dot(place[2 * j + 1], lower)
-        total = part if total is None else total + part
-    return total
+        parts.append(jnp.where(lane >= shifts[j], x, 0.0).astype(BF16))
+        parts.append(jnp.where(lane < shifts[j], x, 0.0).astype(BF16))
+    return _dot(place, jnp.concatenate(parts, axis=0))
 
 
 def reply(field, pick, shifts):
     lane = _iota((L, L), 1)
-    field = field.astype(BF16)
+    found = _dot(pick, field.astype(BF16))
     return [
         jnp.where(
-            lane >= shifts[j], _dot(pick[2 * j], field), _dot(pick[2 * j + 1], field)
+            lane >= shifts[j],
+            found[2 * j * L : (2 * j + 1) * L],
+            found[(2 * j + 1) * L : (2 * j + 2) * L],
         ).astype(BF16)
         for j in range(2)
     ]
@@ -207,7 +207,7 @@
 
 
 def take_reply(got, get, shift):
-    turned = _dot(get[0], got[0]) + _dot(get[1], got[1])
+    turned = _dot(get, jnp.concatenate(got, axis=0))
     return _rotate(turned.astype(BF16), ((L - shift) & 127).astype(jnp.int16)).astype(F32)
 
 
@@ -254,8 +254,7 @@
     tile_row = _as_row(tile_ref[...], scratch)
     offset_row = _as_row(offset_ref[...], scratch)
     get, put_2, put_4, shift = block_tables(tile_row, offset_row)
-    for j in range(2):
-        get_ref[j] = get[j]
+    get_ref[...] = jnp.concatenate(get, axis=1)
     put_2_ref[...] = put_2
     put_4_ref[...] = put_4
     shift_ref[...] = shift
@@ -312,9 +311,8 @@
     message_ref[0] = replies[0]
     message_ref[1] = replies[1]
     message_ref[2] = jnp.broadcast_to(edge_row(field), (L, L)).astype(BF16)
-    for k in range(4):
-        pick_ref[k] = pick[k]
-        place_ref[k] = place[k]
+    pick_ref[...] = pick
+    place_ref[...] = place
     for j in range(2):
         shift_ref[j] = shifts[j]
 
@@ -323,7 +321,7 @@
     got_ref, get_ref, put_ref, shift_ref, normal_ref, field_ref, neighbour_ref, message_ref, foot_ref, prior_ref, back
 ):
     shift = shift_ref[...]
-    foot = take_reply((got_ref[0], got_ref[1]), (get_ref[0], get_ref[1]), shift)
+    foot = take_reply((got_ref[0], got_ref[1]), get_ref[...], shift)
     foot_ref[...] = foot
     turned = apply_normal(normal_ref, foot, back)
     message_ref[...] = send_back(turned, put_ref[...], shift).astype(BF16)
@@ -333,8 +331,8 @@
 
 def middle_kernel(got_ref, field_ref, smooth_ref, pick_ref, place_ref, shift_ref, image_ref, message_ref):
     field = field_ref[...]
-    pick = [pick_ref[k] for k in range(4)]
-    place = [place_ref[k] for k in range(4)]
+    pick = pick_ref[...]
+    place = place_ref[...]
     shifts = [shift_ref[j] for j in range(2)]
     image = add_up((got_ref[0], got_ref[1]), place, shifts) + smooth_ref[...]
     replies = reply(image, pick, shifts)
@@ -357,7 +355,7 @@
     sums = jnp.sum(got_ref[2].astype(F32), axis=0, keepdims=True)
     sums_ref[...] = sums
     step = _whole(sums, SCALARS) / _whole(sums, SCALARS + 3)
-    taken = take_reply((got_ref[0], got_ref[1]), (get_ref[0], get_ref[1]), shift)
+    taken = take_reply((got_ref[0], got_ref[1]), get_ref[...], shift)
     foot = (foot_ref[...] - step * taken).astype(BF16).astype(F32)
     image = image_ref[...]
     before, after = outer_edges(got_ref[2], neighbour_ref[...])
@@ -374,7 +372,7 @@
 
 
 def last_kernel(got_ref, place_ref, shift_ref, field_ref, image_ref, residual_ref, smooth_ref, sums_ref, solution_ref, rest_ref):
-    place = [place_ref[k] for k in range(4)]
+    place = place_ref[...]
     shifts = [shift_ref[j] for j in range(2)]
     residual = residual_ref[...]
     field = field_ref[...]
@@ -448,7 +446,7 @@
         [
             _shape((4 * L, L), BF16),
             pltpu.VMEM((L // 4, 2 * FOOT, 2 * FOOT), BF16),
-            _shape((2, L, L), BF16),
+            _shape((L, 2 * L), BF16),
             _shape((2 * L, L), BF16),
             _shape((4 * L, L), BF16),
             _shape((L, L), jnp.int32),
@@ -482,7 +480,7 @@
 
     field, message, pick, place, shifts = whole_call(
         start_kernel,
-        [WIDE, _shape((3, L, L), BF16), _shape((4, L, L), BF16), _shape((4, L, L), BF16), _shape((2, L, L), jnp.int32)],
+        [WIDE, _shape((3, L, L), BF16), _shape((4 * L, L), BF16), _shape((L, 4 * L), BF16), _shape((2, L, L), jnp.int32)],
         (got,),
     )
     got = exchange(message)

time: 87.1 us -> 87 us (level)
  no operation moved by 1% of the time
where the time goes in v9:
time: 87 us; the launch traced here: 86.8 us
  blocking collectives  75.7 us (87%)
  Pallas kernels  10.1 us (12%)
    all_to_all x3, blocking collectives, exchange_rows(): lax.all_to_all(x.reshape(L, -1, L), SEND, split_axis=0, concat_axis=0, ti...  48.2 us
    all_to_all x2, blocking collectives, exchange(): return lax.all_to_all(x, SEND, split_axis=1, concat_axis=1, tiled=True)  27.5 us
    pallas_call x6, Pallas kernels, call(): pl.pallas_call(kernel, grid=grid, in_specs=in_specs, out_specs=out_specs,...  10.1 us

profile of v9, /device:TPU:1, one launch (start us, length us, event | category | flops | bytes accessed | tf_op | source)
XLA Modules:
  0.0 86.8 jit_solution(13051770660054255247)
XLA Ops:
  0.6 0.0 copy-start
  0.6 5.4 %shard_map.77 = (bf16[512,128]{1,0:T(8,128)(2,1)S(1)}, bf16[32,256,256]{2,1,0:T(8,128)(2,1)S(1)}, bf16[128,256]{1,0:T(8,128)(2,1)S(1)}, bf16[256,128]{1,0:T(8,12...) custom-call(s32[2,64]{1,0:T(2,128)} %tile_hbm.1, s32[2,64]{1,0:T(2,128)} %offset_hbm.1, ...), custom_call_target="tpu_custom_call" | custom-call | flops 1073741824 | bytes 8388608 | tf_op jit(solution)/shard_map/pallas_call | solution.py:407
  6.0 21.3 %all_to_all.25 = bf16[128,4,128]{2,1,0:T(4,128)(2,1)S(1)} all-to-all(bf16[128,4,128]{2,1,0:T(4,128)(2,1)S(1)} %bitcast.20), channel_id=1, replica_groups=mesh['det'=4,'tm_0'=4,'tm_1'=4,'tm_2'=2] {'tm_2','tm_1','tm_0','det'}, dimensions={0} | all-to-all | bytes 262144 | tf_op jit(solution)/shard_map/all_to_all | solution.py:435
  27.4 0.5 shard_map.78
  27.9 0.1 copy.12
  28.0 13.7 %all_to_all.26 = bf16[3,128,128]{2,0,1:T(4,128)(2,1)S(1)} all-to-all(bf16[3,128,128]{2,0,1:T(4,128)(2,1)S(1)} %copy.12), channel_id=1, replica_groups=mesh['det'=4,'tm_0'=4,'tm_1'=4,'tm_2'=2] {'tm_2','tm_1','tm_0','det'}, dimensions={1} | all-to-all | bytes 196608 | tf_op jit(solution)/shard_map/all_to_all | solution.py:431
  41.6 0.0 copy-done
  41.7 1.5 %shard_map.79 = (bf16[256,128]{1,0:T(8,128)(2,1)S(1)}, f32[128,128]{1,0:T(8,128)S(1)}, f32[128,128]{1,0:T(8,128)S(1)}) custom-call(bf16[3,128,128]{2,1,0:T(8,128)(2,1)S(1)} %copy.13.got_ref, bf16[128,256]{1,0:T(8,128)(2,1)S(1)} %get-tuple-element.24.get_ref, bf16[256,128]{1,0:T(8,128)(2,1)S(1)} %get-tuple-element.25.put_ref, ...), custom_call_target="tpu_custom_call" | custom-call | flops 268435456 | bytes 4194304 | tf_op jit(solution)/shard_map/pallas_call | solution.py:407
  43.2 13.2 %all_to_all.27 = bf16[128,2,128]{2,1,0:T(2,128)(2,1)S(1)} all-to-all(bf16[128,2,128]{2,1,0:T(2,128)(2,1)S(1)} %bitcast.21), channel_id=1, replica_groups=mesh['det'=4,'tm_0'=4,'tm_1'=4,'tm_2'=2] {'tm_2','tm_1','tm_0','det'}, dimensions={0} | all-to-all | bytes 131072 | tf_op jit(solution)/shard_map/all_to_all | solution.py:435
  56.3 0.4 shard_map.80
  56.7 0.1 copy.15
  56.8 13.8 %all_to_all.28 = bf16[3,128,128]{2,0,1:T(4,128)(2,1)S(1)} all-to-all(bf16[3,128,128]{2,0,1:T(4,128)(2,1)S(1)} %copy.15), channel_id=1, replica_groups=mesh['det'=4,'tm_0'=4,'tm_1'=4,'tm_2'=2] {'tm_2','tm_1','tm_0','det'}, dimensions={1} | all-to-all | bytes 196608 | tf_op jit(solution)/shard_map/all_to_all | solution.py:431
  70.7 1.6 %shard_map.81 = (bf16[512,128]{1,0:T(8,128)(2,1)S(1)}, f32[128,128]{1,0:T(8,128)S(1)}, f32[128,128]{1,0:T(8,128)S(1)}, f32[1,128]{1,0:T(1,128)S(1)}) custom-call(bf16[3,128,128]{2,1,0:T(8,128)(2,1)S(1)} %copy.16.got_ref, bf16[128,256]{1,0:T(8,128)(2,1)S(1)} %get-tuple-element.24.get_ref, bf16[512,128]{1,0:T(8,128)(2,1)S(1)} %get-tuple-element.35.put_ref, ...), custom_call_target="tpu_custom_call" | custom-call | flops 268435456 | bytes 4194304 | tf_op jit(solution)/shard_map/pallas_call | solution.py:407
  72.3 13.7 %all_to_all.29 = bf16[128,4,128]{2,1,0:T(4,128)(2,1)S(1)} all-to-all(bf16[128,4,128]{2,1,0:T(4,128)(2,1)S(1)} %bitcast.19), channel_id=1, replica_groups=mesh['det'=4,'tm_0'=4,'tm_1'=4,'tm_2'=2] {'tm_2','tm_1','tm_0','det'}, dimensions={0} | all-to-all | bytes 262144 | tf_op jit(solution)/shard_map/all_to_all | solution.py:435
  86.0 0.8 shard_map.82
  (5 shorter events, 0.1 us)
Async XLA Ops:
  0.6 41.0 %copy-start = (s32[16,2]{0,1:T(2,128)S(1)}, s32[16,2]{0,1:T(2,128)}, u32[]{:S(2)}) copy-start(s32[16,2]{0,1:T(2,128)} %param.11) | copy-start | bytes 388
